TPU v7x, 32 devices: a whole 2x2x4 slice. The times are simulated.
32 devices in a mesh: lon: 8 (over z, core), head: 4 (over y, x).
Axes of the slice: x: 2, y: 2, z: 4, core: 2. Of those that a mesh axis runs over, the one named last changes fastest.
Arguments:
- image_tokens: bfloat16 [64, 128, 3072], P(None, 'lon'), may hold values from -6 to 6
- conditioning: bfloat16 [3072], replicated, may hold values from -6 to 6
- mod_weight: bfloat16 [3072, 3, 3072], P(('lon', 'head')), may hold values from -0.21875 to 0.21875
- mod_bias: bfloat16 [3, 3072], replicated, may hold values from -3 to 3
- qkv_weight: bfloat16 [3072, 3, 3072], P('lon', None, 'head'), may hold values from -0.109375 to 0.109375
- qkv_bias: bfloat16 [3, 3072], P(None, 'head'), may hold values from -3 to 3
- q_gain: float32 [128], replicated, may hold values from 0.5 to 12
- k_gain: float32 [128], replicated, may hold values from 0.5 to 12
- text_kv: bfloat16 [2, 512, 3072], P(None, 'lon', 'head'), may hold values from -6 to 6
- proj_weight: bfloat16 [3072, 3072], P('lon', 'head'), may hold values from -0.109375 to 0.109375
- proj_bias: bfloat16 [3072], replicated, may hold values from -3 to 3
Outputs:
- block_output: bfloat16 [64, 128, 3072], P(None, 'lon', 'head')
All inputs are finite; a program needn't handle non-finite values.
Results may differ from a plain program's by a relative error of at most 0.0109.
The roundings to bfloat16 on the way count: a program that leaves them out, or rounds other values in their place, can miss the bound.
Values may be sent and summed in bfloat16 or wider, within the bound.
A program may use at most 128 MiB of HBM per device.

v0:
```python
import math

import jax
import jax.numpy as jnp
from jax import lax
from jax.sharding import PartitionSpec as P

RADIUS = 15
QROWS = 16


def padded_2(cells, sides, width):
    for axis, dim in sides:
        count = lax.axis_size(axis)
        head = lax.slice_in_dim(cells, 0, width, axis=dim)
        tail = lax.slice_in_dim(cells, cells.shape[dim] - width, cells.shape[dim], axis=dim)
        cells = jnp.concatenate(
            [
                lax.ppermute(tail, axis, [(i, (i + 1) % count) for i in range(count)]),
                cells,
                lax.ppermute(head, axis, [((i + 1) % count, i) for i in range(count)]),
            ],
            axis=dim,
        )
    return cells


def rms_scale(entries, gain):
    mean_square = jnp.mean(entries * entries, axis=-1, keepdims=True)
    return entries * lax.rsqrt(mean_square + 1e-06) * gain


def window_mask(row_first, q_rows, q_cols, k_rows, k_cols, lat_total):
    query_index = jnp.arange(q_rows * q_cols, dtype=jnp.int32)
    key_index = jnp.arange(k_rows * k_cols, dtype=jnp.int32)
    query_row = (query_index // q_cols)[:, None]
    query_col = (query_index % q_cols)[:, None]
    key_row = (key_index // k_cols)[None, :]
    key_col = (key_index % k_cols)[None, :]
    global_row = row_first + key_row - RADIUS
    near_rows = jnp.abs(key_row - RADIUS - query_row) <= RADIUS
    near_cols = jnp.abs(key_col - RADIUS - query_col) <= RADIUS
    inside = (global_row >= 0) & (global_row < lat_total)
    return near_rows & near_cols & inside


def attend(queries, key_block, value_block, text_keys, text_values, row_first, lat_total):
    q_rows, q_cols, heads_here, head_dim = queries.shape
    k_rows, k_cols = (key_block.shape[0], key_block.shape[1])
    flat_query = queries.reshape(q_rows * q_cols, heads_here, head_dim)
    flat_keys = key_block.reshape(k_rows * k_cols, heads_here, head_dim)
    flat_values = value_block.reshape(k_rows * k_cols, heads_here, head_dim)
    factor = 1.0 / math.sqrt(head_dim)
    image_scores = (
        jnp.einsum("qhd,khd->hqk", flat_query, flat_keys, preferred_element_type=jnp.float32)
        * factor
    )
    text_scores = (
        jnp.einsum("qhd,khd->hqk", flat_query, text_keys, preferred_element_type=jnp.float32)
        * factor
    )
    allowed = window_mask(row_first, q_rows, q_cols, k_rows, k_cols, lat_total)
    image_scores = jnp.where(allowed[None], image_scores, -jnp.inf)
    highest = jnp.maximum(
        jnp.max(image_scores, axis=2, keepdims=True), jnp.max(text_scores, axis=2, keepdims=True)
    )
    image_exp = jnp.exp(image_scores - highest)
    text_exp = jnp.exp(text_scores - highest)
    normaliser = jnp.sum(image_exp, axis=2, keepdims=True) + jnp.sum(
        text_exp, axis=2, keepdims=True
    )
    image_probs = (image_exp / normaliser).astype(jnp.bfloat16)
    text_probs = (text_exp / normaliser).astype(jnp.bfloat16)
    combined = jnp.einsum(
        "hqk,khd->qhd", image_probs, flat_values, preferred_element_type=jnp.float32
    )
    combined = combined + jnp.einsum(
        "hqk,khd->qhd", text_probs, text_values, preferred_element_type=jnp.float32
    )
    return combined.astype(jnp.bfloat16).reshape(q_rows, q_cols, heads_here * head_dim)


def body(
    image_tokens,
    conditioning,
    mod_weight,
    mod_bias,
    qkv_weight,
    qkv_bias,
    q_gain,
    k_gain,
    text_kv,
    proj_weight,
    proj_bias,
):
    lat_rows, col_count, model_width = image_tokens.shape
    token_count = lat_rows * col_count
    head_groups = lax.axis_size("head")
    slice_rows = mod_weight.shape[0]
    row_offset = (lax.axis_index("lon") * head_groups + lax.axis_index("head")) * slice_rows
    silu_part = jax.nn.silu(
        lax.dynamic_slice_in_dim(conditioning, row_offset, slice_rows, 0).astype(jnp.float32)
    )
    partial_mod = jnp.dot(
        silu_part,
        mod_weight.reshape(slice_rows, 3 * model_width).astype(jnp.float32),
        precision=lax.Precision.HIGHEST,
    )
    modulation = lax.psum(partial_mod, ("lon", "head")).reshape(3, model_width) + mod_bias.astype(
        jnp.float32
    )
    token_values = image_tokens.reshape(token_count, model_width).astype(jnp.float32)
    average = jnp.mean(token_values, axis=1, keepdims=True)
    centred = token_values - average
    variance = jnp.mean(centred * centred, axis=1, keepdims=True)
    modulated = (
        (1.0 + modulation[1]) * (centred * lax.rsqrt(variance + 1e-06)) + modulation[0]
    ).astype(jnp.bfloat16)
    local_inner = qkv_weight.shape[2]
    head_dim = q_gain.shape[0]
    local_heads = local_inner // head_dim
    shard_rows = lax.all_gather(qkv_weight, "lon", axis=0, tiled=True)
    row_total = shard_rows.shape[0]
    projected = jnp.dot(
        modulated,
        shard_rows.reshape(row_total, 3 * local_inner),
        preferred_element_type=jnp.float32,
    )
    projected = projected.reshape(token_count, 3, local_inner) + qkv_bias.astype(jnp.float32)
    queries = rms_scale(
        projected[:, 0].reshape(lat_rows, col_count, local_heads, head_dim), q_gain
    ).astype(jnp.bfloat16)
    keys_normed = rms_scale(
        projected[:, 1].reshape(lat_rows, col_count, local_heads, head_dim), k_gain
    ).astype(jnp.bfloat16)
    values_image = projected[:, 2].astype(jnp.bfloat16).reshape(lat_rows, col_count, local_inner)
    key_value = jnp.stack(
        [keys_normed.reshape(lat_rows, col_count, local_inner), values_image], axis=2
    )
    widened = padded_2(key_value, (("lon", 1),), RADIUS)
    padded = jnp.pad(widened, ((RADIUS, RADIUS), (0, 0), (0, 0), (0, 0)))
    text_panel = lax.all_gather(text_kv, "lon", axis=1, tiled=True)
    text_count = text_panel.shape[1]
    text_keys = text_panel[0].reshape(text_count, local_heads, head_dim)
    text_values = text_panel[1].reshape(text_count, local_heads, head_dim)
    key_cols = col_count + 2 * RADIUS

    def one_block(block_index):
        row_first = block_index * QROWS
        query_block = lax.dynamic_slice_in_dim(queries, row_first, QROWS, 0)
        pair_block = lax.dynamic_slice_in_dim(padded, row_first, QROWS + 2 * RADIUS, 0)
        key_block = pair_block[:, :, 0].reshape(QROWS + 2 * RADIUS, key_cols, local_heads, head_dim)
        value_block = pair_block[:, :, 1].reshape(
            QROWS + 2 * RADIUS, key_cols, local_heads, head_dim
        )
        return attend(
            query_block, key_block, value_block, text_keys, text_values, row_first, lat_rows
        )

    attended = lax.map(one_block, jnp.arange(lat_rows // QROWS, dtype=jnp.int32)).reshape(
        token_count, local_inner
    )
    out_cols = model_width // head_groups
    col_offset = lax.axis_index("head") * out_cols
    proj_columns = lax.all_gather(proj_weight, "lon", axis=0, tiled=True)
    own_rows = lax.all_to_all(proj_columns, "head", split_axis=0, concat_axis=1, tiled=True)
    partial_out = jnp.dot(attended, own_rows, preferred_element_type=jnp.float32)
    out_sum = lax.psum_scatter(partial_out, "head", scatter_dimension=1, tiled=True)
    own_image = lax.dynamic_slice_in_dim(
        image_tokens.reshape(token_count, model_width), col_offset, out_cols, 1
    ).astype(jnp.float32)
    own_gate = lax.dynamic_slice_in_dim(modulation[2], col_offset, out_cols, 0)
    own_bias = lax.dynamic_slice_in_dim(proj_bias, col_offset, out_cols, 0).astype(jnp.float32)
    block_output = (own_image + own_gate * (out_sum + own_bias)).astype(jnp.bfloat16)
    return block_output.reshape(lat_rows, col_count, out_cols)


def solution(mesh):
    placed = (
        P(None, "lon", None),
        P(),
        P(("lon", "head"), None, None),
        P(),
        P("lon", None, "head"),
        P(None, "head"),
        P(),
        P(),
        P(None, "lon", "head"),
        P("lon", "head"),
        P(),
    )
    return jax.shard_map(
        body, mesh=mesh, in_specs=placed, out_specs=P(None, "lon", "head"), check_vma=False
    )
```

profile of v0, /device:TPU:0, one launch (start us, length us, event | category | flops | bytes accessed | tf_op | source)
XLA Modules:
  0.0 694.7 jit_solution(13399464902569084253)
XLA Ops:
  13.9 45.9 %psum.7 = f32[3,3072]{1,0:T(4,128)S(1)} all-reduce(f32[3,3072]{1,0:T(4,128)S(1)} %reshape.296), channel_id=1, replica_groups=mesh['lon'=8,'head'=4] {'lon','head'}, use_global_device_ids=true, to_apply=%region_0.1 | all-reduce | flops 9216 | bytes 73728 | tf_op jit(solution)/shard_map/psum | solution.py:109
  82.4 112.0 %all-gather.4.cloned.1.call-done = bf16[3072,3,768]{0,2,1:T(8,128)(2,1)} async-done(((bf16[384,3,768]{0,2,1:T(8,128)(2,1)}), bf16[3072,3,768]{0,2,1:T(8,128)(2,1)}) %all-gather.4.cloned.1.call-update) | async-done | bytes 14155792 | tf_op jit(solution)/shard_map/all_gather | solution.py:122
  194.4 19.7 %broadcast_add_fusion.1 = f32[1024,3,768]{2,0,1:T(8,128)S(1)} fusion(f32[3,768]{1,0:T(4,128)S(1)} %convert_element_type.84, bf16[1024,3072,1]{1,0,2:T(8,128)(2,1)} %bitcast.83, bf16[3072,3,768]{0,2,1:T(8,128)(2,1)} %all-gather.4.cloned.1.call-done), kind=kOutput, calls=%fused_computation.69 | convolution fusion | flops 14497873920 | bytes 29893632 | tf_op jit(solution)/shard_map/dot_general | solution.py:124
  290.2 18.0 %collective-permute-done = bf16[64,15,2,768]{3,0,2,1:T(8,128)(2,1)} collective-permute-done((bf16[64,15,2,768]{3,0,2,1:T(8,128)(2,1)}, bf16[64,15,2,768]{3,0,2,1:T(8,128)(2,1)}, u32[]{:S(2)}, u32[]{:S(2)}) %collective-permute-start) | collective-permute-done | bytes 2949152 | tf_op jit(solution)/shard_map/ppermute | solution.py:19
  315.2 18.1 %select_maximum_fusion = bf16[94,46,2,768]{3,1,0,2:T(8,128)(2,1)} fusion(bf16[64,15,2,768]{3,1,0,2:T(8,128)(2,1)S(1)} %copy.85, bf16[64,15,2,768]{3,1,0,2:T(8,128)(2,1)S(1)} %copy.84, bf16[64,16,1,768]{3,1,0,2:T(8,128)(2,1)S(1)} %bitcast.80, bf16[64,16,1,768]{3,1,0,2:T(8,128)(2,1)S(1)} %multiply_convert_fusion.1), kind=kLoop, calls=%fused_computation.60 | loop fusion | flops 99624960 | bytes 22327296 | tf_op jit(solution)/shard_map/concatenate | solution.py:17
  333.3 221.7 %while.13 = (s32[]{:T(128)}, bf16[4,16,16,768]{3,2,1,0:T(8,128)(2,1)}, s32[4]{0:T(128)S(1)}, bf16[94,46,2,768]{3,1,0,2:T(8,128)(2,1)}, bf16[64,16,6,128]{3,1,0,2...) while((s32[]{:T(128)}, ...), condition=%wide.region_10.11_spmd, body=%wide.region_5.10_spmd.sunk | while | flops 2117607168 | bytes 124344392 | solution.py:160
  339.9 7.7 %squeeze.25 = bf16[2116,6,128]{2,1,0:T(8,128)(2,1)} reshape(bf16[46,46,1,768]{3,1,0,2:T(8,128)(2,1)} %get-tuple-element.266) | data formatting | bytes 6500352 | tf_op jit(solution)/shard_map/while/body/eval_jaxpr/reshape;while/body/eval_jaxpr/reshape;while/body/eval_jaxpr/squeeze | solution.py:51
  350.6 9.4 %fusion.82 = (f32[6,256]{1,0:T(8,128)S(1)}, f32[6,256,2116]{1,2,0:T(8,128)}) fusion(pred[256,2116]{0,1:T(8,128)(4,1)S(1)} %fusion.81, bf16[256,6,128]{2,0,1:T(8,128)(2,1)S(1)} %bitcast.77, bf16[2116,6,128]{2,1,0:T(8,128)(2,1)} %squeeze.25), kind=kOutput, calls=%fused_computation.3.clone.1 | convolution fusion | flops 841794048 | bytes 17191936 | tf_op jit(solution)/shard_map/while/body/eval_jaxpr/qhd,khd->hqk/dot_general | solution.py:55
  363.3 7.4 %fusion.83 = f32[6,256]{1,0:T(8,128)S(1)} fusion(f32[6,256,2116]{1,2,0:T(8,128)} %get-tuple-element.267, f32[6,256]{1,0:T(8,128)S(1)} %max.13, pred[256,2116]{0,1:T(8,128)(4,1)S(1)} %fusion.81), kind=kLoop, calls=%fused_computation.4.clone.1 | loop fusion | flops 12999168 | bytes 13554688 | tf_op jit(solution)/shard_map/while/body/eval_jaxpr/reduce_sum | solution.py:69
  375.7 10.1 %fusion.85 = f32[256,6,128]{0,2,1:T(8,128)S(1)} fusion(f32[6,256,2116]{1,2,0:T(8,128)} %get-tuple-element.267, f32[6,256]{1,0:T(8,128)S(1)} %add.300, f32[6,256]{1,0:T(8,128)S(1)} %max.13, pred[256,2116]{0,1:T(8,128)(4,1)} %copy-done.4, bf16[2116,6,128]{2,1,0:T(8,128)(2,1)} %squeeze.26), kind=kOutput, calls=%fused_computation.19.clone.1 | convolution fusion | flops 848295936 | bytes 17591296 | tf_op jit(solution)/shard_map/while/body/eval_jaxpr/hqk,khd->qhd/dot_general | solution.py:74
  395.3 7.7 %squeeze.25 = bf16[2116,6,128]{2,1,0:T(8,128)(2,1)} reshape(bf16[46,46,1,768]{3,1,0,2:T(8,128)(2,1)} %get-tuple-element.266) | data formatting | bytes 6500352 | tf_op jit(solution)/shard_map/while/body/eval_jaxpr/reshape;while/body/eval_jaxpr/reshape;while/body/eval_jaxpr/squeeze | solution.py:51
  406.0 9.4 %fusion.82 = (f32[6,256]{1,0:T(8,128)S(1)}, f32[6,256,2116]{1,2,0:T(8,128)}) fusion(pred[256,2116]{0,1:T(8,128)(4,1)S(1)} %fusion.81, bf16[256,6,128]{2,0,1:T(8,128)(2,1)S(1)} %bitcast.77, bf16[2116,6,128]{2,1,0:T(8,128)(2,1)} %squeeze.25), kind=kOutput, calls=%fused_computation.3.clone.1 | convolution fusion | flops 841794048 | bytes 17191936 | tf_op jit(solution)/shard_map/while/body/eval_jaxpr/qhd,khd->hqk/dot_general | solution.py:55
  418.7 7.4 %fusion.83 = f32[6,256]{1,0:T(8,128)S(1)} fusion(f32[6,256,2116]{1,2,0:T(8,128)} %get-tuple-element.267, f32[6,256]{1,0:T(8,128)S(1)} %max.13, pred[256,2116]{0,1:T(8,128)(4,1)S(1)} %fusion.81), kind=kLoop, calls=%fused_computation.4.clone.1 | loop fusion | flops 12999168 | bytes 13554688 | tf_op jit(solution)/shard_map/while/body/eval_jaxpr/reduce_sum | solution.py:69
  431.1 10.1 %fusion.85 = f32[256,6,128]{0,2,1:T(8,128)S(1)} fusion(f32[6,256,2116]{1,2,0:T(8,128)} %get-tuple-element.267, f32[6,256]{1,0:T(8,128)S(1)} %add.300, f32[6,256]{1,0:T(8,128)S(1)} %max.13, pred[256,2116]{0,1:T(8,128)(4,1)} %copy-done.4, bf16[2116,6,128]{2,1,0:T(8,128)(2,1)} %squeeze.26), kind=kOutput, calls=%fused_computation.19.clone.1 | convolution fusion | flops 848295936 | bytes 17591296 | tf_op jit(solution)/shard_map/while/body/eval_jaxpr/hqk,khd->qhd/dot_general | solution.py:74
  450.7 7.7 %squeeze.25 = bf16[2116,6,128]{2,1,0:T(8,128)(2,1)} reshape(bf16[46,46,1,768]{3,1,0,2:T(8,128)(2,1)} %get-tuple-element.266) | data formatting | bytes 6500352 | tf_op jit(solution)/shard_map/while/body/eval_jaxpr/reshape;while/body/eval_jaxpr/reshape;while/body/eval_jaxpr/squeeze | solution.py:51
  461.4 9.4 %fusion.82 = (f32[6,256]{1,0:T(8,128)S(1)}, f32[6,256,2116]{1,2,0:T(8,128)}) fusion(pred[256,2116]{0,1:T(8,128)(4,1)S(1)} %fusion.81, bf16[256,6,128]{2,0,1:T(8,128)(2,1)S(1)} %bitcast.77, bf16[2116,6,128]{2,1,0:T(8,128)(2,1)} %squeeze.25), kind=kOutput, calls=%fused_computation.3.clone.1 | convolution fusion | flops 841794048 | bytes 17191936 | tf_op jit(solution)/shard_map/while/body/eval_jaxpr/qhd,khd->hqk/dot_general | solution.py:55
  474.1 7.4 %fusion.83 = f32[6,256]{1,0:T(8,128)S(1)} fusion(f32[6,256,2116]{1,2,0:T(8,128)} %get-tuple-element.267, f32[6,256]{1,0:T(8,128)S(1)} %max.13, pred[256,2116]{0,1:T(8,128)(4,1)S(1)} %fusion.81), kind=kLoop, calls=%fused_computation.4.clone.1 | loop fusion | flops 12999168 | bytes 13554688 | tf_op jit(solution)/shard_map/while/body/eval_jaxpr/reduce_sum | solution.py:69
  486.5 10.1 %fusion.85 = f32[256,6,128]{0,2,1:T(8,128)S(1)} fusion(f32[6,256,2116]{1,2,0:T(8,128)} %get-tuple-element.267, f32[6,256]{1,0:T(8,128)S(1)} %add.300, f32[6,256]{1,0:T(8,128)S(1)} %max.13, pred[256,2116]{0,1:T(8,128)(4,1)} %copy-done.4, bf16[2116,6,128]{2,1,0:T(8,128)(2,1)} %squeeze.26), kind=kOutput, calls=%fused_computation.19.clone.1 | convolution fusion | flops 848295936 | bytes 17591296 | tf_op jit(solution)/shard_map/while/body/eval_jaxpr/hqk,khd->qhd/dot_general | solution.py:74
  506.1 7.7 %squeeze.25 = bf16[2116,6,128]{2,1,0:T(8,128)(2,1)} reshape(bf16[46,46,1,768]{3,1,0,2:T(8,128)(2,1)} %get-tuple-element.266) | data formatting | bytes 6500352 | tf_op jit(solution)/shard_map/while/body/eval_jaxpr/reshape;while/body/eval_jaxpr/reshape;while/body/eval_jaxpr/squeeze | solution.py:51
  516.8 9.4 %fusion.82 = (f32[6,256]{1,0:T(8,128)S(1)}, f32[6,256,2116]{1,2,0:T(8,128)}) fusion(pred[256,2116]{0,1:T(8,128)(4,1)S(1)} %fusion.81, bf16[256,6,128]{2,0,1:T(8,128)(2,1)S(1)} %bitcast.77, bf16[2116,6,128]{2,1,0:T(8,128)(2,1)} %squeeze.25), kind=kOutput, calls=%fused_computation.3.clone.1 | convolution fusion | flops 841794048 | bytes 17191936 | tf_op jit(solution)/shard_map/while/body/eval_jaxpr/qhd,khd->hqk/dot_general | solution.py:55
  529.5 7.4 %fusion.83 = f32[6,256]{1,0:T(8,128)S(1)} fusion(f32[6,256,2116]{1,2,0:T(8,128)} %get-tuple-element.267, f32[6,256]{1,0:T(8,128)S(1)} %max.13, pred[256,2116]{0,1:T(8,128)(4,1)S(1)} %fusion.81), kind=kLoop, calls=%fused_computation.4.clone.1 | loop fusion | flops 12999168 | bytes 13554688 | tf_op jit(solution)/shard_map/while/body/eval_jaxpr/reduce_sum | solution.py:69
  541.9 10.1 %fusion.85 = f32[256,6,128]{0,2,1:T(8,128)S(1)} fusion(f32[6,256,2116]{1,2,0:T(8,128)} %get-tuple-element.267, f32[6,256]{1,0:T(8,128)S(1)} %add.300, f32[6,256]{1,0:T(8,128)S(1)} %max.13, pred[256,2116]{0,1:T(8,128)(4,1)} %copy-done.4, bf16[2116,6,128]{2,1,0:T(8,128)(2,1)} %squeeze.26), kind=kOutput, calls=%fused_computation.19.clone.1 | convolution fusion | flops 848295936 | bytes 17591296 | tf_op jit(solution)/shard_map/while/body/eval_jaxpr/hqk,khd->qhd/dot_general | solution.py:74
  555.0 10.2 %fusion.54 = f32[1024,3072]{1,0:T(8,128)} fusion(bf16[1024,768]{1,0:T(8,128)(2,1)} %bitcast.92, bf16[768,3072]{0,1:T(8,128)(2,1)} %bitcast.85), kind=kOutput, calls=%fused_computation.99 | convolution fusion | flops 4831838208 | bytes 18874368 | tf_op jit(solution)/shard_map/dot_general | solution.py:167
  566.7 117.4 %reduce-scatter.2.cloned.1.call-done = f32[1024,768]{1,0:T(8,128)} async-done(((f32[1024,3072]{1,0:T(8,128)}), f32[1024,768]{1,0:T(8,128)}) %reduce-scatter.2.cloned.1.call-update) | async-done | bytes 3145744 | tf_op jit(solution)/shard_map/reduce_scatter | solution.py:168
  (183 shorter events, 198.3 us)
Async XLA Ops:
  6.5 63.3 %copy-start = (f32[128]{0:T(128)S(1)}, f32[128]{0:T(128)}, u32[]{:S(2)}) copy-start(f32[128]{0:T(128)} %param.20) | copy-start | bytes 1540
  6.5 70.6 %all-gather.8.cloned.1.call-start = ((), (), s32[]{:S(2)}) async-start(), calls=%async_computation.4 | async-start | bytes 5308416 | tf_op jit(solution)/shard_map/all_gather | solution.py:165
  7.3 187.1 %all-gather.4.cloned.1.call-start = ((), (), s32[]{:S(2)}) async-start(), calls=%async_computation.2 | async-start | bytes 15925248 | tf_op jit(solution)/shard_map/all_gather | solution.py:122
  11.2 237.4 %all-gather.6.cloned.1.call-start = ((), (), s32[]{:S(2)}) async-start(), calls=%async_computation.3 | async-start | bytes 1769472 | tf_op jit(solution)/shard_map/all_gather | solution.py:142
  59.8 10.1 %slice-start = ((s8[6291456]{0:T(1024)(128)(4,1)}), s8[4194304]{0:T(1024)(128)(4,1)S(1)}, s32[]{:S(2)}) async-start(s8[6291456]{0:T(1024)(128)(4,1)} %bitcast.75), calls=%async_computation.6 | async-start | bytes 8388608
  77.2 190.9 %all-to-all-start = ((bf16[4,768,768]{2,1,0:T(8,128)(2,1)}), bf16[4,768,768]{2,1,0:T(8,128)(2,1)}, u32[]{:S(2)}, u32[]{:S(2)}) async-start(bf16[4,768,768]{2,1,0:T(8,128)(2,1)} %bitcast.84), calls=%async_computation | async-start | bytes 9437184 | tf_op jit(solution)/shard_map/all_to_all | solution.py:166
  82.2 601.9 %reduce-scatter.2.cloned.1.call-start = ((), (), s32[]{:S(2)}) async-start(), calls=%async_computation.5 | async-start | bytes 15728640 | tf_op jit(solution)/shard_map/reduce_scatter | solution.py:168
  241.9 66.3 %collective-permute-start = (bf16[64,15,2,768]{3,0,2,1:T(8,128)(2,1)}, bf16[64,15,2,768]{3,0,2,1:T(8,128)(2,1)}, u32[]{:S(2)}, u32[]{:S(2)}) collective-permute-start(bf16[64,15,2,768]{3,0,2,1:T(8,128)(2,1)} %copy.82), channel_id=1, source_target_pairs={{0,4},{4,8},{8,12},{12,16},{16,20},{20,24},{24,28},{28,0},{1,5},{5... | collective-permute-start | bytes 8847368 | tf_op jit(solution)/shard_map/ppermute | solution.py:19
  244.9 66.8 %collective-permute-start.1 = (bf16[64,15,2,768]{3,0,2,1:T(8,128)(2,1)}, bf16[64,15,2,768]{3,0,2,1:T(8,128)(2,1)}, u32[]{:S(2)}, u32[]{:S(2)}) collective-permute-start(bf16[64,15,2,768]{3,0,2,1:T(8,128)(2,1)} %copy.83), channel_id=1, source_target_pairs={{4,0},{8,4},{12,8},{16,12},{20,16},{24,20},{28,24},{0,28},{5,1},{9... | collective-permute-start | bytes 8847368 | tf_op jit(solution)/shard_map/ppermute | solution.py:21
  350.6 12.7 %copy-start.4 = (pred[256,2116]{0,1:T(8,128)(4,1)}, pred[256,2116]{0,1:T(8,128)(4,1)S(1)}, u32[]{:S(2)}) copy-start(pred[256,2116]{0,1:T(8,128)(4,1)S(1)} %fusion.81) | copy-start | bytes 1625092 | tf_op jit(solution)/shard_map/while
  350.6 9.4 %copy-start.5 = (bf16[512,6,128]{2,0,1:T(8,128)(2,1)S(1)}, bf16[512,6,128]{2,0,1:T(8,128)(2,1)}, u32[]{:S(2)}) copy-start(bf16[512,6,128]{2,0,1:T(8,128)(2,1)} %get-tuple-element.303) | copy-start | bytes 2359300 | tf_op jit(solution)/shard_map/while
  375.7 10.1 %copy-start.3 = (f32[6,256,512]{2,1,0:T(8,128)S(1)}, f32[6,256,512]{2,1,0:T(8,128)}, u32[]{:S(2)}) copy-start(f32[6,256,512]{2,1,0:T(8,128)} %copy-done.2) | copy-start | bytes 9437188 | tf_op jit(solution)/shard_map/while
  375.7 10.1 %copy-start.7 = (bf16[512,6,128]{2,0,1:T(8,128)(2,1)S(1)}, bf16[512,6,128]{2,0,1:T(8,128)(2,1)}, u32[]{:S(2)}) copy-start(bf16[512,6,128]{2,0,1:T(8,128)(2,1)} %get-tuple-element.304) | copy-start | bytes 2359300 | tf_op jit(solution)/shard_map/while
  406.0 12.7 %copy-start.4 = (pred[256,2116]{0,1:T(8,128)(4,1)}, pred[256,2116]{0,1:T(8,128)(4,1)S(1)}, u32[]{:S(2)}) copy-start(pred[256,2116]{0,1:T(8,128)(4,1)S(1)} %fusion.81) | copy-start | bytes 1625092 | tf_op jit(solution)/shard_map/while
  431.1 10.1 %copy-start.3 = (f32[6,256,512]{2,1,0:T(8,128)S(1)}, f32[6,256,512]{2,1,0:T(8,128)}, u32[]{:S(2)}) copy-start(f32[6,256,512]{2,1,0:T(8,128)} %copy-done.2) | copy-start | bytes 9437188 | tf_op jit(solution)/shard_map/while
  431.1 10.1 %copy-start.7 = (bf16[512,6,128]{2,0,1:T(8,128)(2,1)S(1)}, bf16[512,6,128]{2,0,1:T(8,128)(2,1)}, u32[]{:S(2)}) copy-start(bf16[512,6,128]{2,0,1:T(8,128)(2,1)} %get-tuple-element.304) | copy-start | bytes 2359300 | tf_op jit(solution)/shard_map/while
  461.4 12.7 %copy-start.4 = (pred[256,2116]{0,1:T(8,128)(4,1)}, pred[256,2116]{0,1:T(8,128)(4,1)S(1)}, u32[]{:S(2)}) copy-start(pred[256,2116]{0,1:T(8,128)(4,1)S(1)} %fusion.81) | copy-start | bytes 1625092 | tf_op jit(solution)/shard_map/while
  486.5 10.1 %copy-start.3 = (f32[6,256,512]{2,1,0:T(8,128)S(1)}, f32[6,256,512]{2,1,0:T(8,128)}, u32[]{:S(2)}) copy-start(f32[6,256,512]{2,1,0:T(8,128)} %copy-done.2) | copy-start | bytes 9437188 | tf_op jit(solution)/shard_map/while
  486.5 10.1 %copy-start.7 = (bf16[512,6,128]{2,0,1:T(8,128)(2,1)S(1)}, bf16[512,6,128]{2,0,1:T(8,128)(2,1)}, u32[]{:S(2)}) copy-start(bf16[512,6,128]{2,0,1:T(8,128)(2,1)} %get-tuple-element.304) | copy-start | bytes 2359300 | tf_op jit(solution)/shard_map/while
  516.8 12.7 %copy-start.4 = (pred[256,2116]{0,1:T(8,128)(4,1)}, pred[256,2116]{0,1:T(8,128)(4,1)S(1)}, u32[]{:S(2)}) copy-start(pred[256,2116]{0,1:T(8,128)(4,1)S(1)} %fusion.81) | copy-start | bytes 1625092 | tf_op jit(solution)/shard_map/while
  516.8 9.4 %copy-start.5 = (bf16[512,6,128]{2,0,1:T(8,128)(2,1)S(1)}, bf16[512,6,128]{2,0,1:T(8,128)(2,1)}, u32[]{:S(2)}) copy-start(bf16[512,6,128]{2,0,1:T(8,128)(2,1)} %get-tuple-element.303) | copy-start | bytes 2359300 | tf_op jit(solution)/shard_map/while
  541.9 10.1 %copy-start.3 = (f32[6,256,512]{2,1,0:T(8,128)S(1)}, f32[6,256,512]{2,1,0:T(8,128)}, u32[]{:S(2)}) copy-start(f32[6,256,512]{2,1,0:T(8,128)} %copy-done.2) | copy-start | bytes 9437188 | tf_op jit(solution)/shard_map/while
  541.9 10.1 %copy-start.7 = (bf16[512,6,128]{2,0,1:T(8,128)(2,1)S(1)}, bf16[512,6,128]{2,0,1:T(8,128)(2,1)}, u32[]{:S(2)}) copy-start(bf16[512,6,128]{2,0,1:T(8,128)(2,1)} %get-tuple-element.304) | copy-start | bytes 2359300 | tf_op jit(solution)/shard_map/while
  565.2 122.8 %copy-start.1 = (f32[128]{0:T(128)S(1)}, f32[128]{0:T(128)}, u32[]{:S(2)}) copy-start(f32[128]{0:T(128)} %param.20) | copy-start | bytes 1540
  (11 other events, 55.5 us)
Sparse Core Ops, SparseCore 0:
  9.0 55.3 all-gather.7
  66.0 128.2 all-gather.3
  196.0 23.2 all-gather.5
  565.3 118.6 reduce-scatter.1
where the time goes:
time: 704 us; the launch traced here: 695 us
  waiting for transfers between devices  248 us (35%)
  local copies, waits for them, and re-layouts  156 us (22%)
  matrix products  118 us (17%)
  other arithmetic  101 us (14%)
  blocking collectives  45.9 us (7%)
  between operations  13.6 us (2%)
  starting transfers between devices  9.2 us (1%)
    reduce_scatter x1, waiting for transfers between devices, body(): lax.psum_scatter(partial_out, 'head', scatter_dimension=1, tiled=True)  117 us
    all_gather x1, waiting for transfers between devices, body(): shard_rows = lax.all_gather(qkv_weight, 'lon', axis=0, tiled=True)  112 us
    psum x1, blocking collectives, body(): lax.psum(partial_mod, ('lon', 'head')).reshape(3, model_width)  45.9 us
    dot_general x4, matrix products, attend(): jnp.einsum('hqk,khd->qhd', image_probs, flat_values, preferred_element_ty...  40.3 us
    dot_general x4, matrix products, attend(): jnp.einsum('qhd,khd->hqk', flat_query, flat_keys, preferred_element_type=...  37.5 us
    squeeze x4, local copies, waits for them, and re-layouts, attend(): flat_keys = key_block.reshape(k_rows * k_cols, heads_here, head_dim)  30.6 us
    reduce_sum x4, other arithmetic, attend(): jnp.sum(image_exp, axis=2, keepdims=True)  29.7 us
    slice x4, local copies, waits for them, and re-layouts, one_block(): pair_block[:, :, 1]  20.5 us
  transfers between devices with their start and end apart: 7, of which 3 were waited for; matrix products, arithmetic and copies ran while one was open for 17% of the time, Pallas kernels for 0%

commit v1 on v0

v1 whole, which is shorter than its diff:
```python
import functools
import math

import jax
import jax.numpy as jnp
from jax import lax
from jax.experimental import pallas as pl
from jax.experimental.pallas import tpu as pltpu
from jax.sharding import PartitionSpec as P

RADIUS = 15
QROWS = 16
VMEM_LIMIT = 56 * 1024 * 1024


def proj_kernel(normed, head_dim, x_ref, w_ref, b_ref, g_ref, o_ref):
    rows, width = o_ref.shape
    step = min(256, rows)

    def one(i, carry):
        at = pl.ds(pl.multiple_of(i * step, step), step)
        raw = jnp.dot(x_ref[at, :], w_ref[...], preferred_element_type=jnp.float32) + b_ref[...]
        if normed:
            for h in range(width // head_dim):
                cols = slice(h * head_dim, (h + 1) * head_dim)
                entries = raw[:, cols]
                mean_square = jnp.mean(entries * entries, axis=-1, keepdims=True)
                scaled = entries * lax.rsqrt(mean_square + 1e-06) * g_ref[...]
                o_ref[at, cols] = scaled.astype(o_ref.dtype)
        else:
            o_ref[at, :] = raw.astype(o_ref.dtype)
        return carry

    lax.fori_loop(0, rows // step, one, 0)


def project(x, w, first, bias, gain, normed):
    rows, depth = x.shape
    inner, head_dim = bias.shape[0], gain.shape[0]
    width = 2 * head_dim if inner % (2 * head_dim) == 0 else head_dim
    off = first // width
    return pl.pallas_call(
        functools.partial(proj_kernel, normed, head_dim),
        out_shape=jax.ShapeDtypeStruct((rows, inner), jnp.bfloat16),
        grid=(inner // width,),
        in_specs=[
            pl.BlockSpec((rows, depth), lambda j: (0, 0), pipeline_mode=pl.Buffered(1)),
            pl.BlockSpec((depth, width), lambda j: (0, off + j)),
            pl.BlockSpec((1, width), lambda j: (0, j)),
            pl.BlockSpec((1, head_dim), lambda j: (0, 0)),
        ],
        out_specs=pl.BlockSpec((rows, width), lambda j: (0, j)),
        compiler_params=pltpu.CompilerParams(vmem_limit_bytes=VMEM_LIMIT),
        cost_estimate=pl.CostEstimate(
            flops=2 * rows * depth * inner,
            bytes_accessed=2 * (rows * depth + depth * inner + rows * inner),
            transcendentals=0,
        ),
    )(x, w, bias.reshape(1, inner), gain.reshape(1, head_dim))


def attn_kernel(
    q_blocks, row_blocks, cols, q_ref, kc, vc, kl, vl, kr, vr, tk, tv, o_ref, bias_ref
):
    block = QROWS * cols
    head_dim = q_ref.shape[1]
    factor = math.log2(math.e) / math.sqrt(head_dim)

    @pl.when(pl.program_id(0) == 0)
    def _():
        query = lax.broadcasted_iota(jnp.int32, (block, 3 * block), 0)
        key = lax.broadcasted_iota(jnp.int32, (block, 3 * block), 1)
        row_gap = key // cols - QROWS - query // cols
        for side in range(3):
            col_gap = key % cols + (side - 1) * cols - query % cols
            near = (jnp.abs(row_gap) <= RADIUS) & (jnp.abs(col_gap) <= RADIUS)
            bias_ref[side] = jnp.where(near, 0.0, -1e30).astype(jnp.float32)

    contract = (((1,), (1,)), ((), ()))
    for n, qb in enumerate(q_blocks):
        low, high = max(qb - 1, 0), min(qb + 2, row_blocks)
        first = (low - qb + 1) * block
        width = (high - low) * block
        q = q_ref[n * block : (n + 1) * block, :]
        scores = []
        values = []
        for side, (k_ref, v_ref) in enumerate(((kl, vl), (kc, vc), (kr, vr))):
            k = k_ref[low * block : high * block, :]
            s = lax.dot_general(q, k, contract, preferred_element_type=jnp.float32)
            scores.append(s + bias_ref[side, :, first : first + width])
            values.append(v_ref[low * block : high * block, :])
        scores.append(lax.dot_general(q, tk[...], contract, preferred_element_type=jnp.float32))
        values.append(tv[...])
        highest = functools.reduce(
            jnp.maximum, [jnp.max(s, axis=1, keepdims=True) for s in scores]
        )
        total = 0.0
        out = 0.0
        for s, v in zip(scores, values):
            p = jnp.exp2((s - highest) * factor)
            total = total + jnp.sum(p, axis=1, keepdims=True)
            out = out + jnp.dot(p.astype(jnp.bfloat16), v, preferred_element_type=jnp.float32)
        o_ref[n * block : (n + 1) * block, :] = (out / total).astype(o_ref.dtype)


def attend(q, own, left, right, text, head_dim, cols, part, parts):
    rows, inner = q.shape
    block = QROWS * cols
    row_blocks = rows // block
    per = row_blocks // parts
    q_blocks = tuple(range(part * per, (part + 1) * per))
    text_count = text[0].shape[0]
    whole = pl.BlockSpec((rows, head_dim), lambda h: (0, h))
    texts = pl.BlockSpec((text_count, head_dim), lambda h: (0, h))
    pairs = per * block * (9 * block + text_count)
    return pl.pallas_call(
        functools.partial(attn_kernel, q_blocks, row_blocks, cols),
        out_shape=jax.ShapeDtypeStruct((per * block, inner), jnp.bfloat16),
        grid=(inner // head_dim,),
        in_specs=[pl.BlockSpec((per * block, head_dim), lambda h: (part, h))]
        + [whole] * 6
        + [texts] * 2,
        out_specs=pl.BlockSpec((per * block, head_dim), lambda h: (0, h)),
        scratch_shapes=[pltpu.VMEM((3, block, 3 * block), jnp.float32)],
        compiler_params=pltpu.CompilerParams(vmem_limit_bytes=VMEM_LIMIT),
        cost_estimate=pl.CostEstimate(
            flops=4 * pairs * inner,
            bytes_accessed=2 * (6 * rows * inner + 2 * text_count * inner + 2 * per * block * inner),
            transcendentals=pairs * (inner // head_dim),
        ),
    )(q, *own, *left, *right, *text)


def out_kernel(parts, a_ref, w_ref, image_ref, gate_ref, bias_ref, o_ref):
    inner = a_ref.shape[2]
    total = bias_ref[...]
    for g in range(parts):
        total = total + jnp.dot(
            a_ref[g], w_ref[g * inner : (g + 1) * inner, :], preferred_element_type=jnp.float32
        )
    o_ref[...] = (image_ref[...].astype(jnp.float32) + gate_ref[...] * total).astype(o_ref.dtype)


def output(gathered, w, image, first, gate, bias):
    groups, rows, inner = gathered.shape
    cols = w.shape[1]
    step = 256
    off = first // step
    return pl.pallas_call(
        functools.partial(out_kernel, groups),
        out_shape=jax.ShapeDtypeStruct((rows, cols), jnp.bfloat16),
        grid=(rows // step,),
        in_specs=[
            pl.BlockSpec((groups, step, inner), lambda i: (0, i, 0)),
            pl.BlockSpec(w.shape, lambda i: (0, 0), pipeline_mode=pl.Buffered(1)),
            pl.BlockSpec((step, cols), lambda i: (off + i, 0)),
            pl.BlockSpec((1, cols), lambda i: (0, 0)),
            pl.BlockSpec((1, cols), lambda i: (0, 0)),
        ],
        out_specs=pl.BlockSpec((step, cols), lambda i: (i, 0)),
        compiler_params=pltpu.CompilerParams(vmem_limit_bytes=VMEM_LIMIT),
        cost_estimate=pl.CostEstimate(
            flops=2 * rows * groups * inner * cols,
            bytes_accessed=2 * (groups * inner * (rows + cols) + 2 * rows * cols),
            transcendentals=0,
        ),
    )(gathered, w, image, gate.reshape(1, cols), bias.reshape(1, cols))


def body(
    image_tokens,
    conditioning,
    mod_weight,
    mod_bias,
    qkv_weight,
    qkv_bias,
    q_gain,
    k_gain,
    text_kv,
    proj_weight,
    proj_bias,
):
    lat_rows, col_count, model_width = image_tokens.shape
    token_count = lat_rows * col_count
    head_groups = lax.axis_size("head")
    inner_here = qkv_weight.shape[2]
    flat_weight = qkv_weight.reshape(qkv_weight.shape[0], 3 * inner_here)
    kv_rows = lax.all_gather(flat_weight[:, inner_here:], "lon", axis=0, tiled=True)
    q_rows = lax.all_gather(flat_weight[:, :inner_here], "lon", axis=0, tiled=True)
    text_panel = lax.all_gather(text_kv, "lon", axis=1, tiled=True)
    proj_columns = lax.all_gather(proj_weight, "lon", axis=0, tiled=True)
    slice_rows = mod_weight.shape[0]
    row_offset = (lax.axis_index("lon") * head_groups + lax.axis_index("head")) * slice_rows
    silu_part = jax.nn.silu(
        lax.dynamic_slice_in_dim(conditioning, row_offset, slice_rows, 0).astype(jnp.float32)
    )
    partial_mod = jnp.dot(
        silu_part,
        mod_weight.reshape(slice_rows, 3 * model_width).astype(jnp.float32),
        precision=lax.Precision.HIGHEST,
    )
    modulation = lax.psum(partial_mod, ("lon", "head")).reshape(3, model_width) + mod_bias.astype(
        jnp.float32
    )
    token_values = image_tokens.reshape(token_count, model_width).astype(jnp.float32)
    average = jnp.mean(token_values, axis=1, keepdims=True)
    centred = token_values - average
    variance = jnp.mean(centred * centred, axis=1, keepdims=True)
    modulated = (
        (1.0 + modulation[1]) * (centred * lax.rsqrt(variance + 1e-06)) + modulation[0]
    ).astype(jnp.bfloat16)
    local_inner = qkv_weight.shape[2]
    head_dim = q_gain.shape[0]
    bias = qkv_bias.astype(jnp.float32)
    own_k = project(modulated, kv_rows, 0, bias[1], k_gain, True)
    own_v = project(modulated, kv_rows, local_inner, bias[2], k_gain, False)
    count = lax.axis_size("lon")
    up = [(i, (i + 1) % count) for i in range(count)]
    down = [((i + 1) % count, i) for i in range(count)]
    left = (lax.ppermute(own_k, "lon", up), lax.ppermute(own_v, "lon", up))
    right = (lax.ppermute(own_k, "lon", down), lax.ppermute(own_v, "lon", down))
    queries = project(modulated, q_rows, 0, bias[0], q_gain, True)
    out_cols = model_width // head_groups
    col_offset = lax.axis_index("head") * out_cols
    own_image = lax.dynamic_slice_in_dim(
        image_tokens.reshape(token_count, model_width), col_offset, out_cols, 1
    )
    own_gate = lax.dynamic_slice_in_dim(modulation[2], col_offset, out_cols, 0)
    own_bias = lax.dynamic_slice_in_dim(proj_bias, col_offset, out_cols, 0).astype(jnp.float32)
    text = (text_panel[0], text_panel[1])
    parts = 2
    rows = token_count // parts
    outs = []
    for part in range(parts):
        attended = attend(
            queries, (own_k, own_v), left, right, text, head_dim, col_count, part, parts
        )
        gathered = lax.all_gather(attended, "head", axis=0)
        outs.append(output(gathered, proj_columns, own_image, part * rows, own_gate, own_bias))
    block_output = jnp.concatenate(outs, axis=0)
    return block_output.reshape(lat_rows, col_count, out_cols)


def solution(mesh):
    placed = (
        P(None, "lon", None),
        P(),
        P(("lon", "head"), None, None),
        P(),
        P("lon", None, "head"),
        P(None, "head"),
        P(),
        P(),
        P(None, "lon", "head"),
        P("lon", "head"),
        P(),
    )
    return jax.shard_map(
        body, mesh=mesh, in_specs=placed, out_specs=P(None, "lon", "head"), check_vma=False
    )
```

time: 704 us -> 384 us (0.55); the launches traced: 695 us -> 383 us
  local copies, waits for them, and re-layouts: 156 us -> 15.5 us
  matrix products: 118 us -> 1.57 us
  Pallas kernels: 0 us -> 81.4 us
  other arithmetic: 101 us -> 20.4 us
  waiting for transfers between devices: 248 us -> 201 us
    reduce_scatter x1 -> x0, waiting for transfers between devices: 117 us -> none  [body(): lax.psum_scatter(partial_out, 'head', scatter_dimension=1, tiled=True)]
    dot_general x18 -> x0, matrix products: 116 us -> none  [the longest x4 40.3 us: attend(): jnp.einsum('hqk,khd->qhd', image_probs, flat_values, preferred_element_ty...]
    pallas_call x0 -> x7, Pallas kernels: none -> 81.4 us  [the longest x3 35.6 us: project(): pl.pallas_call(functools.partial(proj_kernel, normed, head_dim), out_shap...]
    all_gather x1 -> x4, waiting for transfers between devices: 112 us -> 193 us  [the longest x1 83.7 us: body(): lax.all_gather(flat_weight[:, :inner_here], 'lon', axis=0, tiled=True)]
    squeeze x8 -> x1, local copies, waits for them, and re-layouts: 50.5 us -> 2.72 us  [body(): text = (text_panel[0], text_panel[1])]
    reduce_sum x10 -> x0, other arithmetic: 41.2 us -> none  [the longest x4 29.7 us: attend(): jnp.sum(image_exp, axis=2, keepdims=True)]
    slice x8 -> x3, local copies, waits for them, and re-layouts: 31.6 us -> 0.78 us  [the longest x1 0.6 us: body(): own_v = project(modulated, kv_rows, local_inner, bias[2], k_gain, False)]
    ppermute x2 -> x4, waiting for transfers between devices: 18 us -> 0.01 us  [the longest x2 0.01 us: body(): left = (lax.ppermute(own_k, 'lon', up), lax.ppermute(own_v, 'lon', up))]
  transfers between devices with their start and end apart: 7 -> 10, of which waited for: 3 -> 6; matrix products, arithmetic and copies ran while one was open for 17% -> 8% of each run, Pallas kernels for 0% -> 20%
where the time goes in v1:
time: 384 us; the launch traced here: 383 us
  waiting for transfers between devices  201 us (52%)
  Pallas kernels  81.4 us (21%)
  blocking collectives  45.5 us (12%)
  other arithmetic  20.4 us (5%)
  local copies, waits for them, and re-layouts  15.5 us (4%)
  between operations  13.6 us (4%)
  starting transfers between devices  4.25 us (1%)
    all_gather x1, waiting for transfers between devices, body(): lax.all_gather(flat_weight[:, :inner_here], 'lon', axis=0, tiled=True)  83.7 us
    all_gather x2, waiting for transfers between devices, body(): gathered = lax.all_gather(attended, 'head', axis=0)  83.7 us
    psum x1, blocking collectives, body(): lax.psum(partial_mod, ('lon', 'head')).reshape(3, model_width)  45.5 us
    pallas_call x3, Pallas kernels, project(): pl.pallas_call(functools.partial(proj_kernel, normed, head_dim), out_shap...  35.6 us
    pallas_call x2, Pallas kernels, attend(): pl.pallas_call(functools.partial(attn_kernel, q_blocks, row_blocks, cols)...  32.7 us
    all_gather x1, waiting for transfers between devices, body(): lax.all_gather(flat_weight[:, inner_here:], 'lon', axis=0, tiled=True)  25.3 us
    pallas_call x2, Pallas kernels, output(): pl.pallas_call(functools.partial(out_kernel, groups), out_shape=jax.Shape...  13.1 us
    convert_element_type x1, other arithmetic, body(): modulated = ((1.0 + modulation[1]) * (centred * lax.rsqrt(variance + 1e-0...  8.13 us
  transfers between devices with their start and end apart: 10, of which 6 were waited for; matrix products, arithmetic and copies ran while one was open for 8% of the time, Pallas kernels for 20%

profile of v1, /device:TPU:0, one launch (start us, length us, event | category | flops | bytes accessed | tf_op | source)
XLA Modules:
  0.0 383.1 jit_solution(3734319074614387217)
XLA Ops:
  6.5 2.8 copy.14
  9.4 1.5 copy.18
  13.5 1.6 copy.19
  15.1 1.6 fusion.2
  16.7 3.7 convert_reduce_fusion
  20.5 5.3 %fusion.1 = f32[64,16]{1,0:T(8,128)S(1)} fusion(bf16[64,16,3072]{2,1,0:T(8,128)(2,1)} %param.11, f32[64,16]{1,0:T(8,128)S(1)} %broadcast_multiply_fusion), kind=kLoop, calls=%fused_computation.3 | loop fusion | flops 12581888 | bytes 6299648 | tf_op jit(solution)/shard_map/reduce_sum | solution.py:208
  25.9 45.5 %psum.7 = f32[3,3072]{1,0:T(4,128)S(1)} all-reduce(f32[3,3072]{1,0:T(4,128)S(1)} %reshape.66), channel_id=1, replica_groups=mesh['lon'=8,'head'=4] {'lon','head'}, use_global_device_ids=true, to_apply=%region_0.1 | all-reduce | flops 9216 | bytes 73728 | tf_op jit(solution)/shard_map/psum | solution.py:202
  72.1 8.1 %add_convert_fusion.x_ref = bf16[1024,3072]{1,0:T(8,128)(2,1)} fusion(f32[3072]{0:T(1024)S(1)} %bitcast.29, f32[1024]{0:T(1024)S(1)} %rsqrt.12, f32[1024]{0:T(1024)S(1)} %div.14, f32[3072]{0:T(1024)S(1)} %bitcast.30, bf16[64,16,3072]{2,1,0:T(8,128)(2,1)} %param.11), kind=kLoop, calls=%fused_computation.4 | loop fusion | flops 18874368 | bytes 12615680 | tf_op jit(solution)/shard_map/convert_element_type | solution.py:211
  80.2 25.3 %all-gather.11.cloned.1.call-done.w_ref = bf16[3072,1536]{1,0:T(8,128)(2,1)} async-done(((bf16[384,1536]{1,0:T(8,128)(2,1)}), bf16[3072,1536]{1,0:T(8,128)(2,1)}) %all-gather.11.cloned.1.call-update) | async-done | bytes 9437200 | tf_op jit(solution)/shard_map/all_gather | solution.py:188
  105.5 12.2 %shard_map.110.kc = bf16[1024,768]{1,0:T(8,128)(2,1)} custom-call(bf16[1024,3072]{1,0:T(8,128)(2,1)} %add_convert_fusion.x_ref, bf16[3072,1536]{1,0:T(8,128)(2,1)} %all-gather.11.cloned.1.call-done.w_ref, f32[1,768]{1,0:T(1,128)} %get-tuple-element.11.b_ref, f32[1,128]{1,0:T(1,128)} %bitcast.31), custom_call_target="tpu_custom_call" | custom-call | flops 4831838208 | bytes 12582912 | tf_op jit(solution)/shard_map/pallas_call | solution.py:42
  118.0 11.3 %shard_map.111.vc = bf16[1024,768]{1,0:T(8,128)(2,1)} custom-call(bf16[1024,3072]{1,0:T(8,128)(2,1)} %add_convert_fusion.x_ref, bf16[3072,1536]{1,0:T(8,128)(2,1)} %all-gather.11.cloned.1.call-done.w_ref, f32[1,768]{1,0:T(1,128)} %get-tuple-element.10.b_ref, f32[1,128]{1,0:T(1,128)} %bitcast.32), custom_call_target="tpu_custom_call" | custom-call | flops 4831838208 | bytes 12582912 | tf_op jit(solution)/shard_map/pallas_call | solution.py:42
  129.3 3.5 collective-permute-start.2
  133.7 2.7 slice_bitcast_fusion
  136.4 83.7 %all-gather.9.cloned.1.call-done.w_ref = bf16[3072,768]{1,0:T(8,128)(2,1)} async-done(((bf16[384,768]{1,0:T(8,128)(2,1)}), bf16[3072,768]{1,0:T(8,128)(2,1)}) %all-gather.9.cloned.1.call-update) | async-done | bytes 4718608 | tf_op jit(solution)/shard_map/all_gather | solution.py:189
  220.1 12.1 %shard_map.109.q_ref = bf16[1024,768]{1,0:T(8,128)(2,1)} custom-call(bf16[1024,3072]{1,0:T(8,128)(2,1)} %add_convert_fusion.x_ref, bf16[3072,768]{1,0:T(8,128)(2,1)} %all-gather.9.cloned.1.call-done.w_ref, f32[1,768]{1,0:T(1,128)} %get-tuple-element.12.b_ref, f32[1,128]{1,0:T(1,128)} %bitcast.33), custom_call_target="tpu_custom_call" | custom-call | flops 4831838208 | bytes 12582912 | tf_op jit(solution)/shard_map/pallas_call | solution.py:42
  233.4 16.7 %shard_map.112 = bf16[512,768]{1,0:T(8,128)(2,1)} custom-call(bf16[1024,768]{1,0:T(8,128)(2,1)} %shard_map.109.q_ref, bf16[1024,768]{1,0:T(8,128)(2,1)} %shard_map.110.kc, bf16[1024,768]{1,0:T(8,128)(2,1)} %shard_map.111.vc, bf16[1024,768]{1,0:T(8,128)(2,1)} %copy-done.4, bf16[1024,768]{1,0:T(8,128)(2,1)} %collective-permute-done.1.vl, ...), custom_call_target="tpu_custom_call" | custom-call | flops 4429185024 | bytes 12582912 | tf_op jit(solution)/shard_map/pallas_call | solution.py:116
  250.2 16.0 %shard_map.114 = bf16[512,768]{1,0:T(8,128)(2,1)} custom-call(bf16[1024,768]{1,0:T(8,128)(2,1)} %shard_map.109.q_ref, bf16[1024,768]{1,0:T(8,128)(2,1)} %shard_map.110.kc, bf16[1024,768]{1,0:T(8,128)(2,1)} %shard_map.111.vc, bf16[1024,768]{1,0:T(8,128)(2,1)} %copy-done.4, bf16[1024,768]{1,0:T(8,128)(2,1)} %collective-permute-done.1.vl, ...), custom_call_target="tpu_custom_call" | custom-call | flops 4429185024 | bytes 12582912 | tf_op jit(solution)/shard_map/pallas_call | solution.py:116
  268.1 2.7 constant_dynamic-slice_fusion.1.image_ref
  270.8 6.3 %all-gather.15.cloned.1.call-done.w_ref = bf16[3072,768]{1,0:T(8,128)(2,1)} async-done(((bf16[384,768]{1,0:T(8,128)(2,1)}), bf16[3072,768]{1,0:T(8,128)(2,1)}) %all-gather.15.cloned.1.call-update) | async-done | bytes 4718608 | tf_op jit(solution)/shard_map/all_gather | solution.py:191
  277.1 44.5 %all-gather.17.cloned.1.call-done = bf16[2048,768]{1,0:T(8,128)(2,1)} async-done(((bf16[512,768]{1,0:T(8,128)(2,1)}), bf16[2048,768]{1,0:T(8,128)(2,1)}) %all-gather.17.cloned.1.call-update) | async-done | bytes 3145744 | tf_op jit(solution)/shard_map/all_gather | solution.py:238
  321.6 6.5 %shard_map.113 = bf16[512,768]{1,0:T(8,128)(2,1)} custom-call(bf16[4,512,768]{2,1,0:T(8,128)(2,1)} %bitcast.25, bf16[3072,768]{1,0:T(8,128)(2,1)} %all-gather.15.cloned.1.call-done.w_ref, bf16[1024,768]{1,0:T(8,128)(2,1)} %constant_dynamic-slice_fusion.1.image_ref, f32[1,768]{1,0:T(1,128)} %constant_dynamic-slice_fusion.gate_ref, f32[1,768]{1,0:T(1,128)} %reshape.75.bias_ref), custom_call_target="tpu_custom_call" | custom-call | flops 2415919104 | bytes 9437184 | tf_op jit(solution)/shard_map/pallas_call | solution.py:149
  328.2 39.2 %all-gather.19.cloned.1.call-done = bf16[2048,768]{1,0:T(8,128)(2,1)} async-done(((bf16[512,768]{1,0:T(8,128)(2,1)}), bf16[2048,768]{1,0:T(8,128)(2,1)}) %all-gather.19.cloned.1.call-update) | async-done | bytes 3145744 | tf_op jit(solution)/shard_map/all_gather | solution.py:238
  367.3 6.6 %shard_map.115 = bf16[512,768]{1,0:T(8,128)(2,1)} custom-call(bf16[4,512,768]{2,1,0:T(8,128)(2,1)} %bitcast.26, bf16[3072,768]{1,0:T(8,128)(2,1)} %all-gather.15.cloned.1.call-done.w_ref, bf16[1024,768]{1,0:T(8,128)(2,1)} %constant_dynamic-slice_fusion.1.image_ref, f32[1,768]{1,0:T(1,128)} %constant_dynamic-slice_fusion.gate_ref, f32[1,768]{1,0:T(1,128)} %reshape.75.bias_ref), custom_call_target="tpu_custom_call" | custom-call | flops 2415919104 | bytes 9437184 | tf_op jit(solution)/shard_map/pallas_call | solution.py:149
  373.9 2.4 pad_maximum_fusion
  (44 shorter events, 7.9 us)
Async XLA Ops:
  6.5 99.0 %all-gather.11.cloned.1.call-start = ((), (), s32[]{:S(2)}) async-start(), calls=%async_computation.1 | async-start | bytes 10616832 | tf_op jit(solution)/shard_map/all_gather | solution.py:188
  10.9 122.8 %all-gather.13.cloned.1.call-start = ((), (), s32[]{:S(2)}) async-start(), calls=%async_computation.2 | async-start | bytes 1769472 | tf_op jit(solution)/shard_map/all_gather | solution.py:190
  11.7 208.4 %all-gather.9.cloned.1.call-start = ((), (), s32[]{:S(2)}) async-start(), calls=%async_computation | async-start | bytes 5308416 | tf_op jit(solution)/shard_map/all_gather | solution.py:189
  12.9 264.2 %all-gather.15.cloned.1.call-start = ((), (), s32[]{:S(2)}) async-start(), calls=%async_computation.3 | async-start | bytes 5308416 | tf_op jit(solution)/shard_map/all_gather | solution.py:191
  13.5 308.2 %all-gather.17.cloned.1.call-start = ((), (), s32[]{:S(2)}) async-start(), calls=%async_computation.4 | async-start | bytes 3932160 | tf_op jit(solution)/shard_map/all_gather | solution.py:238
  20.5 50.9 %copy-start.2 = (bf16[3,768]{1,0:T(4,128)(2,1)S(1)}, bf16[3,768]{1,0:T(4,128)(2,1)}, u32[]{:S(2)}) copy-start(bf16[3,768]{1,0:T(4,128)(2,1)} %param.16) | copy-start | bytes 13828
  20.5 51.5 %copy-start.1 = (bf16[3,3072]{1,0:T(4,128)(2,1)S(1)}, bf16[3,3072]{1,0:T(4,128)(2,1)}, u32[]{:S(2)}) copy-start(bf16[3,3072]{1,0:T(4,128)(2,1)} %param.14) | copy-start | bytes 55300
  117.7 114.5 %collective-permute-start = (bf16[1024,768]{1,0:T(8,128)(2,1)}, bf16[1024,768]{1,0:T(8,128)(2,1)S(1)}, u32[]{:S(2)}, u32[]{:S(2)}) collective-permute-start(bf16[1024,768]{1,0:T(8,128)(2,1)} %shard_map.110.kc), channel_id=1, source_target_pairs={{0,4},{4,8},{8,12},{12,16},{16,20},{20,24},{24,28},{28,0},{1,5},{5... | collective-permute-start | bytes 4718600 | tf_op jit(solution)/shard_map/ppermute | solution.py:220
  118.0 11.3 %copy-start.3 = (bf16[1024,768]{1,0:T(8,128)(2,1)S(1)}, bf16[1024,768]{1,0:T(8,128)(2,1)}, u32[]{:S(2)}) copy-start(bf16[1024,768]{1,0:T(8,128)(2,1)} %shard_map.110.kc) | copy-start | bytes 4718596
  129.2 103.0 %collective-permute-start.1 = (bf16[1024,768]{1,0:T(8,128)(2,1)}, bf16[1024,768]{1,0:T(8,128)(2,1)}, u32[]{:S(2)}, u32[]{:S(2)}) collective-permute-start(bf16[1024,768]{1,0:T(8,128)(2,1)} %shard_map.111.vc), channel_id=1, source_target_pairs={{0,4},{4,8},{8,12},{12,16},{16,20},{20,24},{24,28},{28,0},{1,5},{5... | collective-permute-start | bytes 4718600 | tf_op jit(solution)/shard_map/ppermute | solution.py:220
  129.3 103.0 %collective-permute-start.2 = (bf16[1024,768]{1,0:T(8,128)(2,1)S(1)}, bf16[1024,768]{1,0:T(8,128)(2,1)}, u32[]{:S(2)}, u32[]{:S(2)}) collective-permute-start(bf16[1024,768]{1,0:T(8,128)(2,1)S(1)} %copy-done.3), channel_id=1, source_target_pairs={{4,0},{8,4},{12,8},{16,12},{20,16},{24,20},{28,24},{0,28},{5,1},{9... | collective-permute-start | bytes 4718600 | tf_op jit(solution)/shard_map/ppermute | solution.py:221
  132.8 99.5 %collective-permute-start.3 = (bf16[1024,768]{1,0:T(8,128)(2,1)}, bf16[1024,768]{1,0:T(8,128)(2,1)}, u32[]{:S(2)}, u32[]{:S(2)}) collective-permute-start(bf16[1024,768]{1,0:T(8,128)(2,1)} %shard_map.111.vc), channel_id=1, source_target_pairs={{4,0},{8,4},{12,8},{16,12},{20,16},{24,20},{28,24},{0,28},{5,1},{9... | collective-permute-start | bytes 4718600 | tf_op jit(solution)/shard_map/ppermute | solution.py:221
  232.2 1.1 copy-start.4
  250.1 117.2 %all-gather.19.cloned.1.call-start = ((), (), s32[]{:S(2)}) async-start(), calls=%async_computation.5 | async-start | bytes 3932160 | tf_op jit(solution)/shard_map/all_gather | solution.py:238
  367.3 6.6 %copy-start = (bf16[512,768]{1,0:T(8,128)(2,1)S(1)}, bf16[512,768]{1,0:T(8,128)(2,1)}, u32[]{:S(2)}) copy-start(bf16[512,768]{1,0:T(8,128)(2,1)} %shard_map.113) | copy-start | bytes 2359300
Sparse Core Ops, SparseCore 0:
  11.0 94.4 all-gather.10
  107.1 26.4 all-gather.12
  135.3 84.7 all-gather.8
  221.6 55.4 all-gather.14
  278.8 42.7 all-gather.16
  323.3 43.9 all-gather.18

commit v2 on v1

--- a/solution.py
+++ b/solution.py
@@ -131,40 +131,66 @@
     )(q, *own, *left, *right, *text)
 
 
-def out_kernel(parts, a_ref, w_ref, image_ref, gate_ref, bias_ref, o_ref):
-    inner = a_ref.shape[2]
+def out_kernel(groups, me_ref, *refs):
+    a_refs = refs[:groups]
+    w_ref, image_ref, gate_ref, bias_ref = refs[groups : groups + 4]
+    o_ref = refs[-1]
+    inner = a_refs[0].shape[1]
     total = bias_ref[...]
-    for g in range(parts):
+    for k in range(groups):
+        row = pl.multiple_of(peer(me_ref[0], k, groups) * inner, inner)
         total = total + jnp.dot(
-            a_ref[g], w_ref[g * inner : (g + 1) * inner, :], preferred_element_type=jnp.float32
+            a_refs[k][...], w_ref[pl.ds(row, inner), :], preferred_element_type=jnp.float32
         )
     o_ref[...] = (image_ref[...].astype(jnp.float32) + gate_ref[...] * total).astype(o_ref.dtype)
 
 
-def output(gathered, w, image, first, gate, bias):
-    groups, rows, inner = gathered.shape
+def peer(me, k, groups):
+    if groups & (groups - 1) == 0:
+        return me ^ k
+    return (me + k) % groups
+
+
+def exchange(block):
+    groups = lax.axis_size("head")
+    return [block] + [
+        lax.ppermute(block, "head", [(peer(i, k, groups), i) for i in range(groups)])
+        for k in range(1, groups)
+    ]
+
+
+def output(gathered, w, image, first, gate, bias, before):
+    groups = len(gathered)
+    rows, inner = gathered[0].shape
     cols = w.shape[1]
     step = 256
     off = first // step
+    here = pl.BlockSpec((step, cols), lambda i: (off + i, 0))
+    row = pl.BlockSpec((1, cols), lambda i: (0, 0))
+    operands = [lax.axis_index("head").astype(jnp.int32).reshape(1), *gathered, w, image]
+    operands += [gate.reshape(1, cols), bias.reshape(1, cols)]
+    specs = [pl.BlockSpec(memory_space=pltpu.SMEM)]
+    specs += [pl.BlockSpec((step, inner), lambda i: (i, 0))] * groups
+    specs += [pl.BlockSpec(w.shape, lambda i: (0, 0), pipeline_mode=pl.Buffered(1)), here, row, row]
+    aliases = {}
+    if before is not None:
+        aliases = {len(operands): 0}
+        operands.append(before)
+        specs.append(pl.BlockSpec(memory_space=pl.ANY))
     return pl.pallas_call(
         functools.partial(out_kernel, groups),
-        out_shape=jax.ShapeDtypeStruct((rows, cols), jnp.bfloat16),
+        out_shape=jax.ShapeDtypeStruct(image.shape, jnp.bfloat16),
         grid=(rows // step,),
-        in_specs=[
-            pl.BlockSpec((groups, step, inner), lambda i: (0, i, 0)),
-            pl.BlockSpec(w.shape, lambda i: (0, 0), pipeline_mode=pl.Buffered(1)),
-            pl.BlockSpec((step, cols), lambda i: (off + i, 0)),
-            pl.BlockSpec((1, cols), lambda i: (0, 0)),
-            pl.BlockSpec((1, cols), lambda i: (0, 0)),
-        ],
-        out_specs=pl.BlockSpec((step, cols), lambda i: (i, 0)),
+        in_specs=specs,
+        out_specs=here,
+        input_output_aliases=aliases,
         compiler_params=pltpu.CompilerParams(vmem_limit_bytes=VMEM_LIMIT),
         cost_estimate=pl.CostEstimate(
             flops=2 * rows * groups * inner * cols,
             bytes_accessed=2 * (groups * inner * (rows + cols) + 2 * rows * cols),
             transcendentals=0,
         ),
-    )(gathered, w, image, gate.reshape(1, cols), bias.reshape(1, cols))
+    )(*operands)
 
 
 def body(
@@ -185,10 +211,15 @@
     head_groups = lax.axis_size("head")
     inner_here = qkv_weight.shape[2]
     flat_weight = qkv_weight.reshape(qkv_weight.shape[0], 3 * inner_here)
-    kv_rows = lax.all_gather(flat_weight[:, inner_here:], "lon", axis=0, tiled=True)
-    q_rows = lax.all_gather(flat_weight[:, :inner_here], "lon", axis=0, tiled=True)
-    text_panel = lax.all_gather(text_kv, "lon", axis=1, tiled=True)
-    proj_columns = lax.all_gather(proj_weight, "lon", axis=0, tiled=True)
+    gather_rows = functools.partial(lax.all_gather, axis_name="lon", axis=0, tiled=True)
+    k_rows = gather_rows(flat_weight[:, inner_here : 2 * inner_here])
+    v_rows = gather_rows(flat_weight[:, 2 * inner_here :])
+    k_rows, q_here = lax.optimization_barrier((k_rows, flat_weight[:, :inner_here]))
+    q_rows = gather_rows(q_here)
+    v_rows, text_here = lax.optimization_barrier((v_rows, text_kv))
+    text_panel = lax.all_gather(text_here, "lon", axis=1, tiled=True)
+    q_rows, proj_here = lax.optimization_barrier((q_rows, proj_weight))
+    proj_columns = gather_rows(proj_here)
     slice_rows = mod_weight.shape[0]
     row_offset = (lax.axis_index("lon") * head_groups + lax.axis_index("head")) * slice_rows
     silu_part = jax.nn.silu(
@@ -212,8 +243,8 @@
     local_inner = qkv_weight.shape[2]
     head_dim = q_gain.shape[0]
     bias = qkv_bias.astype(jnp.float32)
-    own_k = project(modulated, kv_rows, 0, bias[1], k_gain, True)
-    own_v = project(modulated, kv_rows, local_inner, bias[2], k_gain, False)
+    own_k = project(modulated, k_rows, 0, bias[1], k_gain, True)
+    own_v = project(modulated, v_rows, 0, bias[2], k_gain, False)
     count = lax.axis_size("lon")
     up = [(i, (i + 1) % count) for i in range(count)]
     down = [((i + 1) % count, i) for i in range(count)]
@@ -228,16 +259,19 @@
     own_gate = lax.dynamic_slice_in_dim(modulation[2], col_offset, out_cols, 0)
     own_bias = lax.dynamic_slice_in_dim(proj_bias, col_offset, out_cols, 0).astype(jnp.float32)
     text = (text_panel[0], text_panel[1])
-    parts = 2
+    parts = lat_rows // QROWS
     rows = token_count // parts
-    outs = []
+    blocks = []
     for part in range(parts):
         attended = attend(
             queries, (own_k, own_v), left, right, text, head_dim, col_count, part, parts
         )
-        gathered = lax.all_gather(attended, "head", axis=0)
-        outs.append(output(gathered, proj_columns, own_image, part * rows, own_gate, own_bias))
-    block_output = jnp.concatenate(outs, axis=0)
+        blocks.append(exchange(attended))
+    block_output = None
+    for part, gathered in enumerate(blocks):
+        block_output = output(
+            gathered, proj_columns, own_image, part * rows, own_gate, own_bias, block_output
+        )
     return block_output.reshape(lat_rows, col_count, out_cols)
 
 

time: 384 us -> 413 us (1.076)
  starting transfers between devices: 4.25 us -> 23.1 us
  Pallas kernels: 81.4 us -> 99.2 us
  blocking collectives: 45.5 us -> 40.6 us
    all_gather x6 -> x5, waiting for transfers between devices: 200 us -> 156 us  [the longest x1 52.2 us: body(): k_rows = gather_rows(flat_weight[:, inner_here:2 * inner_here])]
    ppermute x2, waiting for transfers between devices: 0.01 us -> 37.3 us  [body(): left = (lax.ppermute(own_k, 'lon', up), lax.ppermute(own_v, 'lon', up))]
    ppermute x0 -> x12, starting transfers between devices: none -> 15.9 us  [exchange(): lax.ppermute(block, 'head', [(peer(i, k, groups), i) for i in range(group...]
    pallas_call x2 -> x4, Pallas kernels: 32.7 us -> 43.2 us  [attend(): pl.pallas_call(functools.partial(attn_kernel, q_blocks, row_blocks, cols)...]
    pallas_call x2 -> x4, Pallas kernels: 13.1 us -> 20.4 us  [output(): pl.pallas_call(functools.partial(out_kernel, groups), out_shape=jax.Shape...]
    ppermute x0 -> x12, waiting for transfers between devices: none -> 5.04 us  [exchange(): lax.ppermute(block, 'head', [(peer(i, k, groups), i) for i in range(group...]
    psum x1, blocking collectives: 45.5 us -> 40.6 us  [body(): lax.psum(partial_mod, ('lon', 'head')).reshape(3, model_width)]
  transfers between devices with their start and end apart: 10 -> 21, of which waited for: 6 -> 7; matrix products, arithmetic and copies ran while one was open for 8% -> 7% of each run, Pallas kernels for 20% -> 23%
where the time goes in v2:
time: 413 us; the launch traced here: 412 us
  waiting for transfers between devices  200 us (48%)
  Pallas kernels  99.2 us (24%)
  blocking collectives  40.6 us (10%)
  starting transfers between devices  23.1 us (6%)
  other arithmetic  17.4 us (4%)
  local copies, waits for them, and re-layouts  16.7 us (4%)
  between operations  13.3 us (3%)
    all_gather x1, waiting for transfers between devices, body(): k_rows = gather_rows(flat_weight[:, inner_here:2 * inner_here])  52.2 us
    all_gather x1, waiting for transfers between devices, body(): q_rows = gather_rows(q_here)  52.1 us
    all_gather x1, waiting for transfers between devices, body(): v_rows = gather_rows(flat_weight[:, 2 * inner_here:])  52.1 us
    pallas_call x4, Pallas kernels, attend(): pl.pallas_call(functools.partial(attn_kernel, q_blocks, row_blocks, cols)...  43.2 us
    psum x1, blocking collectives, body(): lax.psum(partial_mod, ('lon', 'head')).reshape(3, model_width)  40.6 us
    ppermute x2, waiting for transfers between devices, body(): left = (lax.ppermute(own_k, 'lon', up), lax.ppermute(own_v, 'lon', up))  37.3 us
    pallas_call x3, Pallas kernels, project(): pl.pallas_call(functools.partial(proj_kernel, normed, head_dim), out_shap...  35.6 us
    pallas_call x4, Pallas kernels, output(): pl.pallas_call(functools.partial(out_kernel, groups), out_shape=jax.Shape...  20.4 us
  transfers between devices with their start and end apart: 21, of which 7 were waited for; matrix products, arithmetic and copies ran while one was open for 7% of the time, Pallas kernels for 23%

profile of v2, /device:TPU:0, one launch (start us, length us, event | category | flops | bytes accessed | tf_op | source)
XLA Modules:
  0.0 411.9 jit_solution(6228390872574873249)
XLA Ops:
  6.5 2.8 copy.17
  12.9 52.2 %all-gather.6.cloned.1.call-done.w_ref = bf16[3072,768]{1,0:T(8,128)(2,1)} async-done(((bf16[384,768]{1,0:T(8,128)(2,1)}), bf16[3072,768]{1,0:T(8,128)(2,1)}) %all-gather.6.cloned.1.call-update) | async-done | bytes 4718608 | tf_op jit(solution)/shard_map/all_gather | solution.py:215
  65.2 52.1 %all-gather.10.cloned.1.call-done.w_ref = bf16[3072,768]{1,0:T(8,128)(2,1)} async-done(((bf16[384,768]{1,0:T(8,128)(2,1)}), bf16[3072,768]{1,0:T(8,128)(2,1)}) %all-gather.10.cloned.1.call-update) | async-done | bytes 4718608 | tf_op jit(solution)/shard_map/all_gather | solution.py:216
  117.4 52.1 %all-gather.8.cloned.1.call-done.w_ref = bf16[3072,768]{1,0:T(8,128)(2,1)} async-done(((bf16[384,768]{1,0:T(8,128)(2,1)}), bf16[3072,768]{1,0:T(8,128)(2,1)}) %all-gather.8.cloned.1.call-update) | async-done | bytes 4718608 | tf_op jit(solution)/shard_map/all_gather | solution.py:218
  172.8 3.7 convert_reduce_fusion
  176.6 4.7 %fusion.1 = f32[64,16]{1,0:T(8,128)S(1)} fusion(bf16[64,16,3072]{2,1,0:T(8,128)(2,1)} %param.11, f32[64,16]{1,0:T(8,128)S(1)} %broadcast_multiply_fusion), kind=kLoop, calls=%fused_computation.3 | loop fusion | flops 12581888 | bytes 6299648 | tf_op jit(solution)/shard_map/reduce_sum | solution.py:239
  181.4 40.6 %psum.7 = f32[3,3072]{1,0:T(4,128)S(1)} all-reduce(f32[3,3072]{1,0:T(4,128)S(1)} %reshape.77), channel_id=1, replica_groups=mesh['lon'=8,'head'=4] {'lon','head'}, use_global_device_ids=true, to_apply=%region_0.1 | all-reduce | flops 9216 | bytes 73728 | tf_op jit(solution)/shard_map/psum | solution.py:233
  222.7 8.2 %add_convert_fusion.x_ref = bf16[1024,3072]{1,0:T(8,128)(2,1)} fusion(f32[3072]{0:T(1024)S(1)} %bitcast.25, f32[1024]{0:T(1024)S(1)} %rsqrt.12, f32[1024]{0:T(1024)S(1)} %div.14, f32[3072]{0:T(1024)S(1)} %bitcast.26, bf16[64,16,3072]{2,1,0:T(8,128)(2,1)} %param.11), kind=kLoop, calls=%fused_computation.4 | loop fusion | flops 18874368 | bytes 12615680 | tf_op jit(solution)/shard_map/convert_element_type | solution.py:242
  230.9 12.3 %shard_map.110.kc = bf16[1024,768]{1,0:T(8,128)(2,1)} custom-call(bf16[1024,3072]{1,0:T(8,128)(2,1)} %add_convert_fusion.x_ref, bf16[3072,768]{1,0:T(8,128)(2,1)} %all-gather.6.cloned.1.call-done.w_ref, f32[1,768]{1,0:T(1,128)} %get-tuple-element.26.b_ref, f32[1,128]{1,0:T(1,128)} %bitcast.27), custom_call_target="tpu_custom_call" | custom-call | flops 4831838208 | bytes 12582912 | tf_op jit(solution)/shard_map/pallas_call | solution.py:42
  243.2 3.5 collective-permute-start.2
  246.8 11.1 %shard_map.111.vc = bf16[1024,768]{1,0:T(8,128)(2,1)} custom-call(bf16[1024,3072]{1,0:T(8,128)(2,1)} %add_convert_fusion.x_ref, bf16[3072,768]{1,0:T(8,128)(2,1)} %all-gather.10.cloned.1.call-done.w_ref, f32[1,768]{1,0:T(1,128)} %get-tuple-element.25.b_ref, f32[1,128]{1,0:T(1,128)} %bitcast.28), custom_call_target="tpu_custom_call" | custom-call | flops 4831838208 | bytes 12582912 | tf_op jit(solution)/shard_map/pallas_call | solution.py:42
  257.9 3.5 collective-permute-start.3
  264.1 12.1 %shard_map.109.q_ref = bf16[1024,768]{1,0:T(8,128)(2,1)} custom-call(bf16[1024,3072]{1,0:T(8,128)(2,1)} %add_convert_fusion.x_ref, bf16[3072,768]{1,0:T(8,128)(2,1)} %all-gather.8.cloned.1.call-done.w_ref, f32[1,768]{1,0:T(1,128)} %get-tuple-element.27.b_ref, f32[1,128]{1,0:T(1,128)} %bitcast.29), custom_call_target="tpu_custom_call" | custom-call | flops 4831838208 | bytes 12582912 | tf_op jit(solution)/shard_map/pallas_call | solution.py:42
  276.2 4.6 %collective-permute-done.kl = bf16[1024,768]{1,0:T(8,128)(2,1)S(1)} collective-permute-done((bf16[1024,768]{1,0:T(8,128)(2,1)}, bf16[1024,768]{1,0:T(8,128)(2,1)S(1)}, u32[]{:S(2)}, u32[]{:S(2)}) %collective-permute-start) | collective-permute-done | bytes 1572896 | tf_op jit(solution)/shard_map/ppermute | solution.py:251
  281.9 32.7 %collective-permute-done.1.vl = bf16[1024,768]{1,0:T(8,128)(2,1)} collective-permute-done((bf16[1024,768]{1,0:T(8,128)(2,1)}, bf16[1024,768]{1,0:T(8,128)(2,1)}, u32[]{:S(2)}, u32[]{:S(2)}) %collective-permute-start.1) | collective-permute-done | bytes 1572896 | tf_op jit(solution)/shard_map/ppermute | solution.py:251
  314.6 10.0 %shard_map.115.refs_0_ = bf16[256,768]{1,0:T(8,128)(2,1)} custom-call(bf16[1024,768]{1,0:T(8,128)(2,1)} %shard_map.109.q_ref, bf16[1024,768]{1,0:T(8,128)(2,1)} %shard_map.110.kc, bf16[1024,768]{1,0:T(8,128)(2,1)} %shard_map.111.vc, bf16[1024,768]{1,0:T(8,128)(2,1)} %copy-done, bf16[1024,768]{1,0:T(8,128)(2,1)} %collective-permute-done.1.vl, ...), custom_call_target="tpu_custom_call" | custom-call | flops 2214592512 | bytes 11796480 | tf_op jit(solution)/shard_map/pallas_call | solution.py:116
  328.4 11.6 %shard_map.114.refs_0_ = bf16[256,768]{1,0:T(8,128)(2,1)} custom-call(bf16[1024,768]{1,0:T(8,128)(2,1)} %shard_map.109.q_ref, bf16[1024,768]{1,0:T(8,128)(2,1)} %shard_map.110.kc, bf16[1024,768]{1,0:T(8,128)(2,1)} %shard_map.111.vc, bf16[1024,768]{1,0:T(8,128)(2,1)} %copy-done, bf16[1024,768]{1,0:T(8,128)(2,1)} %collective-permute-done.1.vl, ...), custom_call_target="tpu_custom_call" | custom-call | flops 2214592512 | bytes 11796480 | tf_op jit(solution)/shard_map/pallas_call | solution.py:116
  343.5 11.6 %shard_map.113.refs_0_ = bf16[256,768]{1,0:T(8,128)(2,1)} custom-call(bf16[1024,768]{1,0:T(8,128)(2,1)} %shard_map.109.q_ref, bf16[1024,768]{1,0:T(8,128)(2,1)} %shard_map.110.kc, bf16[1024,768]{1,0:T(8,128)(2,1)} %shard_map.111.vc, bf16[1024,768]{1,0:T(8,128)(2,1)} %copy-done, bf16[1024,768]{1,0:T(8,128)(2,1)} %collective-permute-done.1.vl, ...), custom_call_target="tpu_custom_call" | custom-call | flops 2214592512 | bytes 11796480 | tf_op jit(solution)/shard_map/pallas_call | solution.py:116
  362.3 9.9 %shard_map.112.refs_0_ = bf16[256,768]{1,0:T(8,128)(2,1)} custom-call(bf16[1024,768]{1,0:T(8,128)(2,1)} %shard_map.109.q_ref, bf16[1024,768]{1,0:T(8,128)(2,1)} %shard_map.110.kc, bf16[1024,768]{1,0:T(8,128)(2,1)} %shard_map.111.vc, bf16[1024,768]{1,0:T(8,128)(2,1)} %copy-done, bf16[1024,768]{1,0:T(8,128)(2,1)} %collective-permute-done.1.vl, ...), custom_call_target="tpu_custom_call" | custom-call | flops 2214592512 | bytes 11796480 | tf_op jit(solution)/shard_map/pallas_call | solution.py:116
  378.4 5.1 %shard_map.116.refs_8_ = bf16[1024,768]{1,0:T(8,128)(2,1)} custom-call(s32[1]{0:T(128)} %bitcast.me_ref, bf16[256,768]{1,0:T(8,128)(2,1)} %shard_map.115.refs_0_, bf16[256,768]{1,0:T(8,128)(2,1)} %copy-done.3, bf16[256,768]{1,0:T(8,128)(2,1)} %copy-done.4, bf16[256,768]{1,0:T(8,128)(2,1)} %copy-done.5, ...), custom_call_target="tpu_custom_call" | custom-call | flops 1207959552 | bytes 7077888 | tf_op jit(solution)/shard_map/pallas_call | solution.py:180
  383.5 5.1 %shard_map.117.refs_8_ = bf16[1024,768]{1,0:T(8,128)(2,1)} custom-call(s32[1]{0:T(128)} %bitcast.me_ref, bf16[256,768]{1,0:T(8,128)(2,1)} %shard_map.114.refs_0_, bf16[256,768]{1,0:T(8,128)(2,1)} %copy-done.6, bf16[256,768]{1,0:T(8,128)(2,1)} %copy-done.7, bf16[256,768]{1,0:T(8,128)(2,1)} %copy-done.9, ...), custom_call_target="tpu_custom_call", output_to_operand_aliasing={{}: (9, {})} | custom-call | flops 1207959552 | bytes 7077888 | tf_op jit(solution)/shard_map/pallas_call | solution.py:180
  389.4 5.1 %shard_map.118.refs_8_ = bf16[1024,768]{1,0:T(8,128)(2,1)} custom-call(s32[1]{0:T(128)} %bitcast.me_ref, bf16[256,768]{1,0:T(8,128)(2,1)} %shard_map.113.refs_0_, bf16[256,768]{1,0:T(8,128)(2,1)} %copy-done.8, bf16[256,768]{1,0:T(8,128)(2,1)} %copy-done.10, bf16[256,768]{1,0:T(8,128)(2,1)} %collective-permute-done.9.refs_3_, ...), custom_call_target="tpu_custom_call", output_to_operand_aliasing={{}: (9, {})} | custom-call | flops 1207959552 | bytes 7077888 | tf_op jit(solution)/shard_map/pallas_call | solution.py:180
  394.5 5.0 %collective-permute-done.6.refs_3_ = bf16[256,768]{1,0:T(8,128)(2,1)S(1)} collective-permute-done((bf16[256,768]{1,0:T(8,128)(2,1)}, bf16[256,768]{1,0:T(8,128)(2,1)S(1)}, u32[]{:S(2)}, u32[]{:S(2)}) %collective-permute-start.6) | collective-permute-done | bytes 393248 | tf_op jit(solution)/shard_map/ppermute | solution.py:157
  400.3 5.1 %shard_map.119 = bf16[1024,768]{1,0:T(8,128)(2,1)} custom-call(s32[1]{0:T(128)} %bitcast.me_ref, bf16[256,768]{1,0:T(8,128)(2,1)} %shard_map.112.refs_0_, bf16[256,768]{1,0:T(8,128)(2,1)} %copy-done.11, bf16[256,768]{1,0:T(8,128)(2,1)} %copy-done.12, bf16[256,768]{1,0:T(8,128)(2,1)} %copy-done.13, ...), custom_call_target="tpu_custom_call", output_to_operand_aliasing={{}: (9, {})} | custom-call | flops 1207959552 | bytes 7077888 | tf_op jit(solution)/shard_map/pallas_call | solution.py:180
  (90 shorter events, 33.6 us)
Async XLA Ops:
  6.5 58.6 %all-gather.6.cloned.1.call-start = ((), (), s32[]{:S(2)}) async-start(), calls=%async_computation | async-start | bytes 5308416 | tf_op jit(solution)/shard_map/all_gather | solution.py:215
  10.6 106.8 %all-gather.10.cloned.1.call-start = ((), (), s32[]{:S(2)}) async-start(), calls=%async_computation.2 | async-start | bytes 5308416 | tf_op jit(solution)/shard_map/all_gather | solution.py:216
  11.8 157.8 %all-gather.8.cloned.1.call-start = ((), (), s32[]{:S(2)}) async-start(), calls=%async_computation.1 | async-start | bytes 5308416 | tf_op jit(solution)/shard_map/all_gather | solution.py:218
  65.2 196.3 %all-gather.12.cloned.1.call-start = ((), (), s32[]{:S(2)}) async-start(), calls=%async_computation.3 | async-start | bytes 1769472 | tf_op jit(solution)/shard_map/all_gather | solution.py:220
  117.4 261.0 %all-gather.14.cloned.1.call-start = ((), (), s32[]{:S(2)}) async-start(), calls=%async_computation.4 | async-start | bytes 5308416 | tf_op jit(solution)/shard_map/all_gather | solution.py:222
  176.5 45.6 %copy-start.15 = (bf16[3,768]{1,0:T(4,128)(2,1)S(1)}, bf16[3,768]{1,0:T(4,128)(2,1)}, u32[]{:S(2)}) copy-start(bf16[3,768]{1,0:T(4,128)(2,1)} %param.16) | copy-start | bytes 13828
  176.5 46.2 %copy-start.14 = (bf16[3,3072]{1,0:T(4,128)(2,1)S(1)}, bf16[3,3072]{1,0:T(4,128)(2,1)}, u32[]{:S(2)}) copy-start(bf16[3,3072]{1,0:T(4,128)(2,1)} %param.14) | copy-start | bytes 55300
  243.2 37.6 %collective-permute-start = (bf16[1024,768]{1,0:T(8,128)(2,1)}, bf16[1024,768]{1,0:T(8,128)(2,1)S(1)}, u32[]{:S(2)}, u32[]{:S(2)}) collective-permute-start(bf16[1024,768]{1,0:T(8,128)(2,1)} %shard_map.110.kc), channel_id=1, source_target_pairs={{0,4},{4,8},{8,12},{12,16},{16,20},{20,24},{24,28},{28,0},{1,5},{5... | collective-permute-start | bytes 4718600 | tf_op jit(solution)/shard_map/ppermute | solution.py:251
  243.2 38.7 %collective-permute-start.2 = (bf16[1024,768]{1,0:T(8,128)(2,1)}, bf16[1024,768]{1,0:T(8,128)(2,1)S(1)}, u32[]{:S(2)}, u32[]{:S(2)}) collective-permute-start(bf16[1024,768]{1,0:T(8,128)(2,1)} %shard_map.110.kc), channel_id=1, source_target_pairs={{4,0},{8,4},{12,8},{16,12},{20,16},{24,20},{28,24},{0,28},{5,1},{9... | collective-permute-start | bytes 4718600 | tf_op jit(solution)/shard_map/ppermute | solution.py:252
  257.9 56.7 %collective-permute-start.1 = (bf16[1024,768]{1,0:T(8,128)(2,1)}, bf16[1024,768]{1,0:T(8,128)(2,1)}, u32[]{:S(2)}, u32[]{:S(2)}) collective-permute-start(bf16[1024,768]{1,0:T(8,128)(2,1)} %shard_map.111.vc), channel_id=1, source_target_pairs={{0,4},{4,8},{8,12},{12,16},{16,20},{20,24},{24,28},{28,0},{1,5},{5... | collective-permute-start | bytes 4718600 | tf_op jit(solution)/shard_map/ppermute | solution.py:251
  257.9 56.7 %collective-permute-start.3 = (bf16[1024,768]{1,0:T(8,128)(2,1)}, bf16[1024,768]{1,0:T(8,128)(2,1)}, u32[]{:S(2)}, u32[]{:S(2)}) collective-permute-start(bf16[1024,768]{1,0:T(8,128)(2,1)} %shard_map.111.vc), channel_id=1, source_target_pairs={{4,0},{8,4},{12,8},{16,12},{20,16},{24,20},{28,24},{0,28},{5,1},{9... | collective-permute-start | bytes 4718600 | tf_op jit(solution)/shard_map/ppermute | solution.py:252
  280.8 33.8 %copy-start = (bf16[1024,768]{1,0:T(8,128)(2,1)}, bf16[1024,768]{1,0:T(8,128)(2,1)S(1)}, u32[]{:S(2)}) copy-start(bf16[1024,768]{1,0:T(8,128)(2,1)S(1)} %collective-permute-done.kl) | copy-start | bytes 4718596
  324.6 30.5 %collective-permute-start.13 = (bf16[256,768]{1,0:T(8,128)(2,1)}, bf16[256,768]{1,0:T(8,128)(2,1)S(1)}, u32[]{:S(2)}, u32[]{:S(2)}) collective-permute-start(bf16[256,768]{1,0:T(8,128)(2,1)} %shard_map.115.refs_0_), channel_id=1, source_target_pairs={{1,0},{0,1},{3,2},{2,3},{5,4},{4,5},{7,6},{6,7},{9,8},{8,9},{11,10... | collective-permute-start | bytes 1179656 | tf_op jit(solution)/shard_map/ppermute | solution.py:157
  326.8 28.4 %collective-permute-start.14 = (bf16[256,768]{1,0:T(8,128)(2,1)}, bf16[256,768]{1,0:T(8,128)(2,1)S(1)}, u32[]{:S(2)}, u32[]{:S(2)}) collective-permute-start(bf16[256,768]{1,0:T(8,128)(2,1)} %shard_map.115.refs_0_), channel_id=1, source_target_pairs={{2,0},{3,1},{0,2},{1,3},{6,4},{7,5},{4,6},{5,7},{10,8},{11,9},{8,1... | collective-permute-start | bytes 1179656 | tf_op jit(solution)/shard_map/ppermute | solution.py:157
  328.3 32.4 %collective-permute-start.15 = (bf16[256,768]{1,0:T(8,128)(2,1)}, bf16[256,768]{1,0:T(8,128)(2,1)S(1)}, u32[]{:S(2)}, u32[]{:S(2)}) collective-permute-start(bf16[256,768]{1,0:T(8,128)(2,1)} %shard_map.115.refs_0_), channel_id=1, source_target_pairs={{3,0},{2,1},{1,2},{0,3},{7,4},{6,5},{5,6},{4,7},{11,8},{10,9},{9,1... | collective-permute-start | bytes 1179656 | tf_op jit(solution)/shard_map/ppermute | solution.py:157
  340.0 22.1 %collective-permute-start.10 = (bf16[256,768]{1,0:T(8,128)(2,1)}, bf16[256,768]{1,0:T(8,128)(2,1)S(1)}, u32[]{:S(2)}, u32[]{:S(2)}) collective-permute-start(bf16[256,768]{1,0:T(8,128)(2,1)} %shard_map.114.refs_0_), channel_id=1, source_target_pairs={{1,0},{0,1},{3,2},{2,3},{5,4},{4,5},{7,6},{6,7},{9,8},{8,9},{11,10... | collective-permute-start | bytes 1179656 | tf_op jit(solution)/shard_map/ppermute | solution.py:157
  342.0 30.2 %collective-permute-start.11 = (bf16[256,768]{1,0:T(8,128)(2,1)}, bf16[256,768]{1,0:T(8,128)(2,1)S(1)}, u32[]{:S(2)}, u32[]{:S(2)}) collective-permute-start(bf16[256,768]{1,0:T(8,128)(2,1)} %shard_map.114.refs_0_), channel_id=1, source_target_pairs={{2,0},{3,1},{0,2},{1,3},{6,4},{7,5},{4,6},{5,7},{10,8},{11,9},{8,1... | collective-permute-start | bytes 1179656 | tf_op jit(solution)/shard_map/ppermute | solution.py:157
  355.1 19.1 %collective-permute-start.12 = (bf16[256,768]{1,0:T(8,128)(2,1)S(1)}, bf16[256,768]{1,0:T(8,128)(2,1)S(1)}, u32[]{:S(2)}, u32[]{:S(2)}) collective-permute-start(bf16[256,768]{1,0:T(8,128)(2,1)S(1)} %copy-done.2), channel_id=1, source_target_pairs={{3,0},{2,1},{1,2},{0,3},{7,4},{6,5},{5,6},{4,7},{11,8},{10,9},{9,1... | collective-permute-start | bytes 1179656 | tf_op jit(solution)/shard_map/ppermute | solution.py:157
  355.3 20.4 %collective-permute-start.7 = (bf16[256,768]{1,0:T(8,128)(2,1)}, bf16[256,768]{1,0:T(8,128)(2,1)S(1)}, u32[]{:S(2)}, u32[]{:S(2)}) collective-permute-start(bf16[256,768]{1,0:T(8,128)(2,1)} %shard_map.113.refs_0_), channel_id=1, source_target_pairs={{1,0},{0,1},{3,2},{2,3},{5,4},{4,5},{7,6},{6,7},{9,8},{8,9},{11,10... | collective-permute-start | bytes 1179656 | tf_op jit(solution)/shard_map/ppermute | solution.py:157
  360.7 28.0 %collective-permute-start.8 = (bf16[256,768]{1,0:T(8,128)(2,1)}, bf16[256,768]{1,0:T(8,128)(2,1)S(1)}, u32[]{:S(2)}, u32[]{:S(2)}) collective-permute-start(bf16[256,768]{1,0:T(8,128)(2,1)} %shard_map.113.refs_0_), channel_id=1, source_target_pairs={{2,0},{3,1},{0,2},{1,3},{6,4},{7,5},{4,6},{5,7},{10,8},{11,9},{8,1... | collective-permute-start | bytes 1179656 | tf_op jit(solution)/shard_map/ppermute | solution.py:157
  362.1 26.5 %collective-permute-start.9 = (bf16[256,768]{1,0:T(8,128)(2,1)}, bf16[256,768]{1,0:T(8,128)(2,1)}, u32[]{:S(2)}, u32[]{:S(2)}) collective-permute-start(bf16[256,768]{1,0:T(8,128)(2,1)} %shard_map.113.refs_0_), channel_id=1, source_target_pairs={{3,0},{2,1},{1,2},{0,3},{7,4},{6,5},{5,6},{4,7},{11,8},{10,9},{9,1... | collective-permute-start | bytes 1179656 | tf_op jit(solution)/shard_map/ppermute | solution.py:157
  372.3 22.3 %collective-permute-start.4 = (bf16[256,768]{1,0:T(8,128)(2,1)}, bf16[256,768]{1,0:T(8,128)(2,1)S(1)}, u32[]{:S(2)}, u32[]{:S(2)}) collective-permute-start(bf16[256,768]{1,0:T(8,128)(2,1)} %shard_map.112.refs_0_), channel_id=1, source_target_pairs={{1,0},{0,1},{3,2},{2,3},{5,4},{4,5},{7,6},{6,7},{9,8},{8,9},{11,10... | collective-permute-start | bytes 1179656 | tf_op jit(solution)/shard_map/ppermute | solution.py:157
  374.2 20.3 %collective-permute-start.5 = (bf16[256,768]{1,0:T(8,128)(2,1)}, bf16[256,768]{1,0:T(8,128)(2,1)S(1)}, u32[]{:S(2)}, u32[]{:S(2)}) collective-permute-start(bf16[256,768]{1,0:T(8,128)(2,1)} %shard_map.112.refs_0_), channel_id=1, source_target_pairs={{2,0},{3,1},{0,2},{1,3},{6,4},{7,5},{4,6},{5,7},{10,8},{11,9},{8,1... | collective-permute-start | bytes 1179656 | tf_op jit(solution)/shard_map/ppermute | solution.py:157
  375.7 23.8 %collective-permute-start.6 = (bf16[256,768]{1,0:T(8,128)(2,1)}, bf16[256,768]{1,0:T(8,128)(2,1)S(1)}, u32[]{:S(2)}, u32[]{:S(2)}) collective-permute-start(bf16[256,768]{1,0:T(8,128)(2,1)} %shard_map.112.refs_0_), channel_id=1, source_target_pairs={{3,0},{2,1},{1,2},{0,3},{7,4},{6,5},{5,6},{4,7},{11,8},{10,9},{9,1... | collective-permute-start | bytes 1179656 | tf_op jit(solution)/shard_map/ppermute | solution.py:157
  (13 other events, 143.5 us)
Sparse Core Ops, SparseCore 0:
  10.7 54.3 all-gather.5
  66.8 50.5 all-gather.9
  119.0 50.5 all-gather.7
  171.0 23.8 all-gather.11
  196.4 51.4 all-gather.13

commit v3 on v2

--- a/solution.py
+++ b/solution.py
@@ -214,12 +214,6 @@
     gather_rows = functools.partial(lax.all_gather, axis_name="lon", axis=0, tiled=True)
     k_rows = gather_rows(flat_weight[:, inner_here : 2 * inner_here])
     v_rows = gather_rows(flat_weight[:, 2 * inner_here :])
-    k_rows, q_here = lax.optimization_barrier((k_rows, flat_weight[:, :inner_here]))
-    q_rows = gather_rows(q_here)
-    v_rows, text_here = lax.optimization_barrier((v_rows, text_kv))
-    text_panel = lax.all_gather(text_here, "lon", axis=1, tiled=True)
-    q_rows, proj_here = lax.optimization_barrier((q_rows, proj_weight))
-    proj_columns = gather_rows(proj_here)
     slice_rows = mod_weight.shape[0]
     row_offset = (lax.axis_index("lon") * head_groups + lax.axis_index("head")) * slice_rows
     silu_part = jax.nn.silu(
@@ -233,6 +227,8 @@
     modulation = lax.psum(partial_mod, ("lon", "head")).reshape(3, model_width) + mod_bias.astype(
         jnp.float32
     )
+    modulation, q_here = lax.optimization_barrier((modulation, flat_weight[:, :inner_here]))
+    q_rows = gather_rows(q_here)
     token_values = image_tokens.reshape(token_count, model_width).astype(jnp.float32)
     average = jnp.mean(token_values, axis=1, keepdims=True)
     centred = token_values - average
@@ -244,7 +240,11 @@
     head_dim = q_gain.shape[0]
     bias = qkv_bias.astype(jnp.float32)
     own_k = project(modulated, k_rows, 0, bias[1], k_gain, True)
+    own_k, text_here = lax.optimization_barrier((own_k, text_kv))
+    text_panel = lax.all_gather(text_here, "lon", axis=1, tiled=True)
     own_v = project(modulated, v_rows, 0, bias[2], k_gain, False)
+    own_v, proj_here = lax.optimization_barrier((own_v, proj_weight))
+    proj_columns = gather_rows(proj_here)
     count = lax.axis_size("lon")
     up = [(i, (i + 1) % count) for i in range(count)]
     down = [((i + 1) % count, i) for i in range(count)]

time: 413 us -> 344 us (0.83)
  waiting for transfers between devices: 200 us -> 126 us
  blocking collectives: 40.6 us -> 45.7 us
    all_gather x1, waiting for transfers between devices: 52.2 us -> 0.01 us  [body(): k_rows = gather_rows(flat_weight[:, inner_here:2 * inner_here])]
    ppermute x2, waiting for transfers between devices: 37.3 us -> 7.09 us  [body(): left = (lax.ppermute(own_k, 'lon', up), lax.ppermute(own_v, 'lon', up))]
    all_gather x1, waiting for transfers between devices: 0.01 us -> 29 us  [body(): text_panel = lax.all_gather(text_here, 'lon', axis=1, tiled=True)]
    all_gather x1, waiting for transfers between devices: 52.1 us -> 26.5 us  [body(): v_rows = gather_rows(flat_weight[:, 2 * inner_here:])]
    all_gather x1, waiting for transfers between devices: 52.1 us -> 61.7 us  [body(): q_rows = gather_rows(q_here)]
    psum x1, blocking collectives: 40.6 us -> 45.7 us  [body(): lax.psum(partial_mod, ('lon', 'head')).reshape(3, model_width)]
  transfers between devices with their start and end apart: 21 -> 21, of which waited for: 7 -> 7; matrix products, arithmetic and copies ran while one was open for 7% -> 9% of each run, Pallas kernels for 23% -> 28%
where the time goes in v3:
time: 344 us; the launch traced here: 343 us
  waiting for transfers between devices  126 us (37%)
  Pallas kernels  99.4 us (29%)
  blocking collectives  45.7 us (13%)
  starting transfers between devices  22.4 us (7%)
  other arithmetic  17.5 us (5%)
  local copies, waits for them, and re-layouts  16.6 us (5%)
  between operations  13.3 us (4%)
    all_gather x1, waiting for transfers between devices, body(): q_rows = gather_rows(q_here)  61.7 us
    psum x1, blocking collectives, body(): lax.psum(partial_mod, ('lon', 'head')).reshape(3, model_width)  45.7 us
    pallas_call x4, Pallas kernels, attend(): pl.pallas_call(functools.partial(attn_kernel, q_blocks, row_blocks, cols)...  43.4 us
    pallas_call x3, Pallas kernels, project(): pl.pallas_call(functools.partial(proj_kernel, normed, head_dim), out_shap...  35.6 us
    all_gather x1, waiting for transfers between devices, body(): text_panel = lax.all_gather(text_here, 'lon', axis=1, tiled=True)  29 us
    all_gather x1, waiting for transfers between devices, body(): v_rows = gather_rows(flat_weight[:, 2 * inner_here:])  26.5 us
    pallas_call x4, Pallas kernels, output(): pl.pallas_call(functools.partial(out_kernel, groups), out_shape=jax.Shape...  20.4 us
    ppermute x12, starting transfers between devices, exchange(): lax.ppermute(block, 'head', [(peer(i, k, groups), i) for i in range(group...  15.1 us
  transfers between devices with their start and end apart: 21, of which 7 were waited for; matrix products, arithmetic and copies ran while one was open for 9% of the time, Pallas kernels for 28%

profile of v3, /device:TPU:0, one launch (start us, length us, event | category | flops | bytes accessed | tf_op | source)
XLA Modules:
  0.0 342.7 jit_solution(10555202108455691206)
XLA Ops:
  6.5 2.8 copy.17
  16.1 45.7 %psum.7 = f32[3,3072]{1,0:T(4,128)S(1)} all-reduce(f32[3,3072]{1,0:T(4,128)S(1)} %reshape.77), channel_id=1, replica_groups=mesh['lon'=8,'head'=4] {'lon','head'}, use_global_device_ids=true, to_apply=%region_0.1 | all-reduce | flops 9216 | bytes 73728 | tf_op jit(solution)/shard_map/psum | solution.py:227
  61.9 3.7 %convert_reduce_fusion = f32[64,16]{1,0:T(8,128)S(1)} fusion(bf16[64,16,3072]{2,1,0:T(8,128)(2,1)} %param.11), kind=kLoop, calls=%fused_computation.1 | loop fusion | flops 6290432 | bytes 6295552 | tf_op jit(solution)/shard_map/reduce_sum | solution.py:233
  65.7 4.5 %fusion.1 = f32[64,16]{1,0:T(8,128)S(1)} fusion(bf16[64,16,3072]{2,1,0:T(8,128)(2,1)} %param.11, f32[64,16]{1,0:T(8,128)S(1)} %broadcast_multiply_fusion), kind=kLoop, calls=%fused_computation.3 | loop fusion | flops 12581888 | bytes 6299648 | tf_op jit(solution)/shard_map/reduce_sum | solution.py:235
  71.0 8.4 %add_convert_fusion.x_ref = bf16[1024,3072]{1,0:T(8,128)(2,1)} fusion(f32[3072]{0:T(1024)S(1)} %bitcast.25, f32[1024]{0:T(1024)S(1)} %rsqrt.12, f32[1024]{0:T(1024)S(1)} %div.14, f32[3072]{0:T(1024)S(1)} %bitcast.26, bf16[64,16,3072]{2,1,0:T(8,128)(2,1)} %param.11), kind=kLoop, calls=%fused_computation.4 | loop fusion | flops 18874368 | bytes 12615680 | tf_op jit(solution)/shard_map/convert_element_type | solution.py:238
  79.4 12.2 %shard_map.110.kc = bf16[1024,768]{1,0:T(8,128)(2,1)} custom-call(bf16[1024,3072]{1,0:T(8,128)(2,1)} %add_convert_fusion.x_ref, bf16[3072,768]{1,0:T(8,128)(2,1)} %all-gather.8.cloned.1.call-done.w_ref, f32[1,768]{1,0:T(1,128)} %get-tuple-element.26.b_ref, f32[1,128]{1,0:T(1,128)} %bitcast.27), custom_call_target="tpu_custom_call" | custom-call | flops 4831838208 | bytes 12582912 | tf_op jit(solution)/shard_map/pallas_call | solution.py:42
  91.7 26.5 %all-gather.10.cloned.1.call-done.w_ref = bf16[3072,768]{1,0:T(8,128)(2,1)} async-done(((bf16[384,768]{1,0:T(8,128)(2,1)}), bf16[3072,768]{1,0:T(8,128)(2,1)}) %all-gather.10.cloned.1.call-update) | async-done | bytes 4718608 | tf_op jit(solution)/shard_map/all_gather | solution.py:216
  118.3 11.2 %shard_map.111.vc = bf16[1024,768]{1,0:T(8,128)(2,1)} custom-call(bf16[1024,3072]{1,0:T(8,128)(2,1)} %add_convert_fusion.x_ref, bf16[3072,768]{1,0:T(8,128)(2,1)} %all-gather.10.cloned.1.call-done.w_ref, f32[1,768]{1,0:T(1,128)} %get-tuple-element.25.b_ref, f32[1,128]{1,0:T(1,128)} %bitcast.28), custom_call_target="tpu_custom_call" | custom-call | flops 4831838208 | bytes 12582912 | tf_op jit(solution)/shard_map/pallas_call | solution.py:42
  129.8 3.3 collective-permute-start.3
  133.1 3.5 %collective-permute-start.2 = (bf16[1024,768]{1,0:T(8,128)(2,1)S(1)}, bf16[1024,768]{1,0:T(8,128)(2,1)}, u32[]{:S(2)}, u32[]{:S(2)}) collective-permute-start(bf16[1024,768]{1,0:T(8,128)(2,1)S(1)} %copy-done), channel_id=1, source_target_pairs={{4,0},{8,4},{12,8},{16,12},{20,16},{24,20},{28,24},{0,28},{5,1},{9... | collective-permute-start | bytes 4718600 | tf_op jit(solution)/shard_map/ppermute | solution.py:252
  136.7 61.7 %all-gather.6.cloned.1.call-done.w_ref = bf16[3072,768]{1,0:T(8,128)(2,1)} async-done(((bf16[384,768]{1,0:T(8,128)(2,1)}), bf16[3072,768]{1,0:T(8,128)(2,1)}) %all-gather.6.cloned.1.call-update) | async-done | bytes 4718608 | tf_op jit(solution)/shard_map/all_gather | solution.py:231
  198.4 12.1 %shard_map.109.q_ref = bf16[1024,768]{1,0:T(8,128)(2,1)} custom-call(bf16[1024,3072]{1,0:T(8,128)(2,1)} %add_convert_fusion.x_ref, bf16[3072,768]{1,0:T(8,128)(2,1)} %all-gather.6.cloned.1.call-done.w_ref, f32[1,768]{1,0:T(1,128)} %get-tuple-element.27.b_ref, f32[1,128]{1,0:T(1,128)} %bitcast.29), custom_call_target="tpu_custom_call" | custom-call | flops 4831838208 | bytes 12582912 | tf_op jit(solution)/shard_map/pallas_call | solution.py:42
  210.6 29.0 %all-gather.12.cloned.1.call-done = bf16[2,512,768]{2,1,0:T(8,128)(2,1)} async-done(((bf16[2,64,768]{2,1,0:T(8,128)(2,1)}), bf16[2,512,768]{2,1,0:T(8,128)(2,1)}) %all-gather.12.cloned.1.call-update) | async-done | bytes 1572880 | tf_op jit(solution)/shard_map/all_gather | solution.py:244
  239.5 2.6 slice_bitcast_fusion
  242.1 7.1 %collective-permute-done.kl = bf16[1024,768]{1,0:T(8,128)(2,1)} collective-permute-done((bf16[1024,768]{1,0:T(8,128)(2,1)S(1)}, bf16[1024,768]{1,0:T(8,128)(2,1)}, u32[]{:S(2)}, u32[]{:S(2)}) %collective-permute-start) | collective-permute-done | bytes 1572896 | tf_op jit(solution)/shard_map/ppermute | solution.py:251
  249.2 10.1 %shard_map.115.refs_0_ = bf16[256,768]{1,0:T(8,128)(2,1)} custom-call(bf16[1024,768]{1,0:T(8,128)(2,1)} %shard_map.109.q_ref, bf16[1024,768]{1,0:T(8,128)(2,1)} %shard_map.110.kc, bf16[1024,768]{1,0:T(8,128)(2,1)} %shard_map.111.vc, bf16[1024,768]{1,0:T(8,128)(2,1)} %collective-permute-done.kl, bf16[1024,768]{1,0:T(8,128)(2,1)} %copy-done.1, ...), custom_call_target="tpu_custom_call" | custom-call | flops 2214592512 | bytes 11796480 | tf_op jit(solution)/shard_map/pallas_call | solution.py:116
  262.8 11.7 %shard_map.114.refs_0_ = bf16[256,768]{1,0:T(8,128)(2,1)} custom-call(bf16[1024,768]{1,0:T(8,128)(2,1)} %shard_map.109.q_ref, bf16[1024,768]{1,0:T(8,128)(2,1)} %shard_map.110.kc, bf16[1024,768]{1,0:T(8,128)(2,1)} %shard_map.111.vc, bf16[1024,768]{1,0:T(8,128)(2,1)} %collective-permute-done.kl, bf16[1024,768]{1,0:T(8,128)(2,1)} %copy-done.1, ...), custom_call_target="tpu_custom_call" | custom-call | flops 2214592512 | bytes 11796480 | tf_op jit(solution)/shard_map/pallas_call | solution.py:116
  277.6 11.6 %shard_map.113.refs_0_ = bf16[256,768]{1,0:T(8,128)(2,1)} custom-call(bf16[1024,768]{1,0:T(8,128)(2,1)} %shard_map.109.q_ref, bf16[1024,768]{1,0:T(8,128)(2,1)} %shard_map.110.kc, bf16[1024,768]{1,0:T(8,128)(2,1)} %shard_map.111.vc, bf16[1024,768]{1,0:T(8,128)(2,1)} %collective-permute-done.kl, bf16[1024,768]{1,0:T(8,128)(2,1)} %copy-done.1, ...), custom_call_target="tpu_custom_call" | custom-call | flops 2214592512 | bytes 11796480 | tf_op jit(solution)/shard_map/pallas_call | solution.py:116
  292.2 2.7 constant_dynamic-slice_fusion.1.refs_5_
  296.9 9.9 %shard_map.112.refs_0_ = bf16[256,768]{1,0:T(8,128)(2,1)} custom-call(bf16[1024,768]{1,0:T(8,128)(2,1)} %shard_map.109.q_ref, bf16[1024,768]{1,0:T(8,128)(2,1)} %shard_map.110.kc, bf16[1024,768]{1,0:T(8,128)(2,1)} %shard_map.111.vc, bf16[1024,768]{1,0:T(8,128)(2,1)} %collective-permute-done.kl, bf16[1024,768]{1,0:T(8,128)(2,1)} %copy-done.1, ...), custom_call_target="tpu_custom_call" | custom-call | flops 2214592512 | bytes 11796480 | tf_op jit(solution)/shard_map/pallas_call | solution.py:116
  312.6 5.1 %shard_map.116.refs_8_ = bf16[1024,768]{1,0:T(8,128)(2,1)} custom-call(s32[1]{0:T(128)} %bitcast.me_ref, bf16[256,768]{1,0:T(8,128)(2,1)} %shard_map.115.refs_0_, bf16[256,768]{1,0:T(8,128)(2,1)} %copy-done.3, bf16[256,768]{1,0:T(8,128)(2,1)} %copy-done.4, bf16[256,768]{1,0:T(8,128)(2,1)} %copy-done.5, ...), custom_call_target="tpu_custom_call" | custom-call | flops 1207959552 | bytes 7077888 | tf_op jit(solution)/shard_map/pallas_call | solution.py:180
  317.7 5.1 %shard_map.117.refs_8_ = bf16[1024,768]{1,0:T(8,128)(2,1)} custom-call(s32[1]{0:T(128)} %bitcast.me_ref, bf16[256,768]{1,0:T(8,128)(2,1)} %shard_map.114.refs_0_, bf16[256,768]{1,0:T(8,128)(2,1)} %copy-done.6, bf16[256,768]{1,0:T(8,128)(2,1)} %copy-done.7, bf16[256,768]{1,0:T(8,128)(2,1)} %copy-done.9, ...), custom_call_target="tpu_custom_call", output_to_operand_aliasing={{}: (9, {})} | custom-call | flops 1207959552 | bytes 7077888 | tf_op jit(solution)/shard_map/pallas_call | solution.py:180
  323.6 5.1 %shard_map.118.refs_8_ = bf16[1024,768]{1,0:T(8,128)(2,1)} custom-call(s32[1]{0:T(128)} %bitcast.me_ref, bf16[256,768]{1,0:T(8,128)(2,1)} %shard_map.113.refs_0_, bf16[256,768]{1,0:T(8,128)(2,1)} %copy-done.8, bf16[256,768]{1,0:T(8,128)(2,1)} %copy-done.10, bf16[256,768]{1,0:T(8,128)(2,1)} %collective-permute-done.9.refs_3_, ...), custom_call_target="tpu_custom_call", output_to_operand_aliasing={{}: (9, {})} | custom-call | flops 1207959552 | bytes 7077888 | tf_op jit(solution)/shard_map/pallas_call | solution.py:180
  331.1 5.1 %shard_map.119 = bf16[1024,768]{1,0:T(8,128)(2,1)} custom-call(s32[1]{0:T(128)} %bitcast.me_ref, bf16[256,768]{1,0:T(8,128)(2,1)} %shard_map.112.refs_0_, bf16[256,768]{1,0:T(8,128)(2,1)} %copy-done.11, bf16[256,768]{1,0:T(8,128)(2,1)} %copy-done.12, bf16[256,768]{1,0:T(8,128)(2,1)} %copy-done.13, ...), custom_call_target="tpu_custom_call", output_to_operand_aliasing={{}: (9, {})} | custom-call | flops 1207959552 | bytes 7077888 | tf_op jit(solution)/shard_map/pallas_call | solution.py:180
  (90 shorter events, 28.4 us)
Async XLA Ops:
  6.5 72.9 %all-gather.8.cloned.1.call-start = ((), (), s32[]{:S(2)}) async-start(), calls=%async_computation.1 | async-start | bytes 5308416 | tf_op jit(solution)/shard_map/all_gather | solution.py:215
  10.6 51.2 %copy-start.14 = (bf16[3,3072]{1,0:T(4,128)(2,1)S(1)}, bf16[3,3072]{1,0:T(4,128)(2,1)}, u32[]{:S(2)}) copy-start(bf16[3,3072]{1,0:T(4,128)(2,1)} %param.14) | copy-start | bytes 55300
  10.6 107.7 %all-gather.10.cloned.1.call-start = ((), (), s32[]{:S(2)}) async-start(), calls=%async_computation.2 | async-start | bytes 5308416 | tf_op jit(solution)/shard_map/all_gather | solution.py:216
  11.8 186.7 %all-gather.6.cloned.1.call-start = ((), (), s32[]{:S(2)}) async-start(), calls=%async_computation | async-start | bytes 5308416 | tf_op jit(solution)/shard_map/all_gather | solution.py:231
  61.8 177.7 %all-gather.12.cloned.1.call-start = ((), (), s32[]{:S(2)}) async-start(), calls=%async_computation.3 | async-start | bytes 1769472 | tf_op jit(solution)/shard_map/all_gather | solution.py:244
  91.7 220.9 %all-gather.14.cloned.1.call-start = ((), (), s32[]{:S(2)}) async-start(), calls=%async_computation.4 | async-start | bytes 5308416 | tf_op jit(solution)/shard_map/all_gather | solution.py:247
  129.5 112.6 %collective-permute-start.1 = (bf16[1024,768]{1,0:T(8,128)(2,1)}, bf16[1024,768]{1,0:T(8,128)(2,1)S(1)}, u32[]{:S(2)}, u32[]{:S(2)}) collective-permute-start(bf16[1024,768]{1,0:T(8,128)(2,1)} %shard_map.111.vc), channel_id=1, source_target_pairs={{0,4},{4,8},{8,12},{12,16},{16,20},{20,24},{24,28},{28,0},{1,5},{5... | collective-permute-start | bytes 4718600 | tf_op jit(solution)/shard_map/ppermute | solution.py:251
  129.8 112.3 %collective-permute-start.3 = (bf16[1024,768]{1,0:T(8,128)(2,1)}, bf16[1024,768]{1,0:T(8,128)(2,1)}, u32[]{:S(2)}, u32[]{:S(2)}) collective-permute-start(bf16[1024,768]{1,0:T(8,128)(2,1)} %shard_map.111.vc), channel_id=1, source_target_pairs={{4,0},{8,4},{12,8},{16,12},{20,16},{24,20},{28,24},{0,28},{5,1},{9... | collective-permute-start | bytes 4718600 | tf_op jit(solution)/shard_map/ppermute | solution.py:252
  133.1 116.1 %collective-permute-start = (bf16[1024,768]{1,0:T(8,128)(2,1)S(1)}, bf16[1024,768]{1,0:T(8,128)(2,1)}, u32[]{:S(2)}, u32[]{:S(2)}) collective-permute-start(bf16[1024,768]{1,0:T(8,128)(2,1)S(1)} %copy-done), channel_id=1, source_target_pairs={{0,4},{4,8},{8,12},{12,16},{16,20},{20,24},{24,28},{28,0},{1,5},{5... | collective-permute-start | bytes 4718600 | tf_op jit(solution)/shard_map/ppermute | solution.py:251
  133.1 116.1 %collective-permute-start.2 = (bf16[1024,768]{1,0:T(8,128)(2,1)S(1)}, bf16[1024,768]{1,0:T(8,128)(2,1)}, u32[]{:S(2)}, u32[]{:S(2)}) collective-permute-start(bf16[1024,768]{1,0:T(8,128)(2,1)S(1)} %copy-done), channel_id=1, source_target_pairs={{4,0},{8,4},{12,8},{16,12},{20,16},{24,20},{28,24},{0,28},{5,1},{9... | collective-permute-start | bytes 4718600 | tf_op jit(solution)/shard_map/ppermute | solution.py:252
  259.3 29.9 %collective-permute-start.13 = (bf16[256,768]{1,0:T(8,128)(2,1)}, bf16[256,768]{1,0:T(8,128)(2,1)S(1)}, u32[]{:S(2)}, u32[]{:S(2)}) collective-permute-start(bf16[256,768]{1,0:T(8,128)(2,1)} %shard_map.115.refs_0_), channel_id=1, source_target_pairs={{1,0},{0,1},{3,2},{2,3},{5,4},{4,5},{7,6},{6,7},{9,8},{8,9},{11,10... | collective-permute-start | bytes 1179656 | tf_op jit(solution)/shard_map/ppermute | solution.py:157
  260.9 29.0 %collective-permute-start.14 = (bf16[256,768]{1,0:T(8,128)(2,1)}, bf16[256,768]{1,0:T(8,128)(2,1)S(1)}, u32[]{:S(2)}, u32[]{:S(2)}) collective-permute-start(bf16[256,768]{1,0:T(8,128)(2,1)} %shard_map.115.refs_0_), channel_id=1, source_target_pairs={{2,0},{3,1},{0,2},{1,3},{6,4},{7,5},{4,6},{5,7},{10,8},{11,9},{8,1... | collective-permute-start | bytes 1179656 | tf_op jit(solution)/shard_map/ppermute | solution.py:157
  262.4 32.6 %collective-permute-start.15 = (bf16[256,768]{1,0:T(8,128)(2,1)}, bf16[256,768]{1,0:T(8,128)(2,1)S(1)}, u32[]{:S(2)}, u32[]{:S(2)}) collective-permute-start(bf16[256,768]{1,0:T(8,128)(2,1)} %shard_map.115.refs_0_), channel_id=1, source_target_pairs={{3,0},{2,1},{1,2},{0,3},{7,4},{6,5},{5,6},{4,7},{11,8},{10,9},{9,1... | collective-permute-start | bytes 1179656 | tf_op jit(solution)/shard_map/ppermute | solution.py:157
  274.6 21.7 %collective-permute-start.10 = (bf16[256,768]{1,0:T(8,128)(2,1)}, bf16[256,768]{1,0:T(8,128)(2,1)S(1)}, u32[]{:S(2)}, u32[]{:S(2)}) collective-permute-start(bf16[256,768]{1,0:T(8,128)(2,1)} %shard_map.114.refs_0_), channel_id=1, source_target_pairs={{1,0},{0,1},{3,2},{2,3},{5,4},{4,5},{7,6},{6,7},{9,8},{8,9},{11,10... | collective-permute-start | bytes 1179656 | tf_op jit(solution)/shard_map/ppermute | solution.py:157
  276.2 30.7 %collective-permute-start.11 = (bf16[256,768]{1,0:T(8,128)(2,1)}, bf16[256,768]{1,0:T(8,128)(2,1)S(1)}, u32[]{:S(2)}, u32[]{:S(2)}) collective-permute-start(bf16[256,768]{1,0:T(8,128)(2,1)} %shard_map.114.refs_0_), channel_id=1, source_target_pairs={{2,0},{3,1},{0,2},{1,3},{6,4},{7,5},{4,6},{5,7},{10,8},{11,9},{8,1... | collective-permute-start | bytes 1179656 | tf_op jit(solution)/shard_map/ppermute | solution.py:157
  289.3 17.6 %copy-start.3 = (bf16[256,768]{1,0:T(8,128)(2,1)}, bf16[256,768]{1,0:T(8,128)(2,1)S(1)}, u32[]{:S(2)}) copy-start(bf16[256,768]{1,0:T(8,128)(2,1)S(1)} %collective-permute-done.13.refs_1_) | copy-start | bytes 1179652
  289.3 19.2 %collective-permute-start.12 = (bf16[256,768]{1,0:T(8,128)(2,1)S(1)}, bf16[256,768]{1,0:T(8,128)(2,1)S(1)}, u32[]{:S(2)}, u32[]{:S(2)}) collective-permute-start(bf16[256,768]{1,0:T(8,128)(2,1)S(1)} %copy-done.2), channel_id=1, source_target_pairs={{3,0},{2,1},{1,2},{0,3},{7,4},{6,5},{5,6},{4,7},{11,8},{10,9},{9,1... | collective-permute-start | bytes 1179656 | tf_op jit(solution)/shard_map/ppermute | solution.py:157
  289.9 16.9 %copy-start.4 = (bf16[256,768]{1,0:T(8,128)(2,1)}, bf16[256,768]{1,0:T(8,128)(2,1)S(1)}, u32[]{:S(2)}) copy-start(bf16[256,768]{1,0:T(8,128)(2,1)S(1)} %collective-permute-done.14.refs_2_) | copy-start | bytes 1179652
  289.9 20.1 %collective-permute-start.7 = (bf16[256,768]{1,0:T(8,128)(2,1)}, bf16[256,768]{1,0:T(8,128)(2,1)S(1)}, u32[]{:S(2)}, u32[]{:S(2)}) collective-permute-start(bf16[256,768]{1,0:T(8,128)(2,1)} %shard_map.113.refs_0_), channel_id=1, source_target_pairs={{1,0},{0,1},{3,2},{2,3},{5,4},{4,5},{7,6},{6,7},{9,8},{8,9},{11,10... | collective-permute-start | bytes 1179656 | tf_op jit(solution)/shard_map/ppermute | solution.py:157
  294.9 27.9 %collective-permute-start.8 = (bf16[256,768]{1,0:T(8,128)(2,1)}, bf16[256,768]{1,0:T(8,128)(2,1)S(1)}, u32[]{:S(2)}, u32[]{:S(2)}) collective-permute-start(bf16[256,768]{1,0:T(8,128)(2,1)} %shard_map.113.refs_0_), channel_id=1, source_target_pairs={{2,0},{3,1},{0,2},{1,3},{6,4},{7,5},{4,6},{5,7},{10,8},{11,9},{8,1... | collective-permute-start | bytes 1179656 | tf_op jit(solution)/shard_map/ppermute | solution.py:157
  296.3 26.6 %collective-permute-start.9 = (bf16[256,768]{1,0:T(8,128)(2,1)}, bf16[256,768]{1,0:T(8,128)(2,1)}, u32[]{:S(2)}, u32[]{:S(2)}) collective-permute-start(bf16[256,768]{1,0:T(8,128)(2,1)} %shard_map.113.refs_0_), channel_id=1, source_target_pairs={{3,0},{2,1},{1,2},{0,3},{7,4},{6,5},{5,6},{4,7},{11,8},{10,9},{9,1... | collective-permute-start | bytes 1179656 | tf_op jit(solution)/shard_map/ppermute | solution.py:157
  306.9 21.8 %collective-permute-start.4 = (bf16[256,768]{1,0:T(8,128)(2,1)}, bf16[256,768]{1,0:T(8,128)(2,1)S(1)}, u32[]{:S(2)}, u32[]{:S(2)}) collective-permute-start(bf16[256,768]{1,0:T(8,128)(2,1)} %shard_map.112.refs_0_), channel_id=1, source_target_pairs={{1,0},{0,1},{3,2},{2,3},{5,4},{4,5},{7,6},{6,7},{9,8},{8,9},{11,10... | collective-permute-start | bytes 1179656 | tf_op jit(solution)/shard_map/ppermute | solution.py:157
  308.5 20.9 %collective-permute-start.5 = (bf16[256,768]{1,0:T(8,128)(2,1)}, bf16[256,768]{1,0:T(8,128)(2,1)S(1)}, u32[]{:S(2)}, u32[]{:S(2)}) collective-permute-start(bf16[256,768]{1,0:T(8,128)(2,1)} %shard_map.112.refs_0_), channel_id=1, source_target_pairs={{2,0},{3,1},{0,2},{1,3},{6,4},{7,5},{4,6},{5,7},{10,8},{11,9},{8,1... | collective-permute-start | bytes 1179656 | tf_op jit(solution)/shard_map/ppermute | solution.py:157
  310.0 20.4 %collective-permute-start.6 = (bf16[256,768]{1,0:T(8,128)(2,1)}, bf16[256,768]{1,0:T(8,128)(2,1)S(1)}, u32[]{:S(2)}, u32[]{:S(2)}) collective-permute-start(bf16[256,768]{1,0:T(8,128)(2,1)} %shard_map.112.refs_0_), channel_id=1, source_target_pairs={{3,0},{2,1},{1,2},{0,3},{7,4},{6,5},{5,6},{4,7},{11,8},{10,9},{9,1... | collective-permute-start | bytes 1179656 | tf_op jit(solution)/shard_map/ppermute | solution.py:157
  (13 other events, 95.9 us)
Sparse Core Ops, SparseCore 0:
  10.7 55.3 all-gather.7
  67.7 50.5 all-gather.9
  119.9 78.4 all-gather.5
  199.9 39.5 all-gather.11
  241.0 54.5 all-gather.13

commit v4 on v3

--- a/solution.py
+++ b/solution.py
@@ -16,10 +16,11 @@
 def proj_kernel(normed, head_dim, x_ref, w_ref, b_ref, g_ref, o_ref):
     rows, width = o_ref.shape
     step = min(256, rows)
+    weight = w_ref[...].reshape(x_ref.shape[1], width)
 
     def one(i, carry):
         at = pl.ds(pl.multiple_of(i * step, step), step)
-        raw = jnp.dot(x_ref[at, :], w_ref[...], preferred_element_type=jnp.float32) + b_ref[...]
+        raw = jnp.dot(x_ref[at, :], weight, preferred_element_type=jnp.float32) + b_ref[...]
         if normed:
             for h in range(width // head_dim):
                 cols = slice(h * head_dim, (h + 1) * head_dim)
@@ -45,7 +46,7 @@
         grid=(inner // width,),
         in_specs=[
             pl.BlockSpec((rows, depth), lambda j: (0, 0), pipeline_mode=pl.Buffered(1)),
-            pl.BlockSpec((depth, width), lambda j: (0, off + j)),
+            pl.BlockSpec((w.shape[0], depth // w.shape[0], width), lambda j: (0, 0, off + j)),
             pl.BlockSpec((1, width), lambda j: (0, j)),
             pl.BlockSpec((1, head_dim), lambda j: (0, 0)),
         ],
@@ -60,22 +61,16 @@
 
 
 def attn_kernel(
-    q_blocks, row_blocks, cols, q_ref, kc, vc, kl, vl, kr, vr, tk, tv, o_ref, bias_ref
+    q_blocks, row_blocks, cols, q_ref, kc, vc, kl, vl, kr, vr, text, bias_ref, o_ref
 ):
     block = QROWS * cols
     head_dim = q_ref.shape[1]
     factor = math.log2(math.e) / math.sqrt(head_dim)
 
-    @pl.when(pl.program_id(0) == 0)
-    def _():
-        query = lax.broadcasted_iota(jnp.int32, (block, 3 * block), 0)
-        key = lax.broadcasted_iota(jnp.int32, (block, 3 * block), 1)
-        row_gap = key // cols - QROWS - query // cols
-        for side in range(3):
-            col_gap = key % cols + (side - 1) * cols - query % cols
-            near = (jnp.abs(row_gap) <= RADIUS) & (jnp.abs(col_gap) <= RADIUS)
-            bias_ref[side] = jnp.where(near, 0.0, -1e30).astype(jnp.float32)
-
+    shards, text_rows, _ = text.shape
+    each = text_rows // 2
+    tk = text[:, :each, :].reshape(shards * each, head_dim)
+    tv = text[:, each:, :].reshape(shards * each, head_dim)
     contract = (((1,), (1,)), ((), ()))
     for n, qb in enumerate(q_blocks):
         low, high = max(qb - 1, 0), min(qb + 2, row_blocks)
@@ -89,8 +84,8 @@
             s = lax.dot_general(q, k, contract, preferred_element_type=jnp.float32)
             scores.append(s + bias_ref[side, :, first : first + width])
             values.append(v_ref[low * block : high * block, :])
-        scores.append(lax.dot_general(q, tk[...], contract, preferred_element_type=jnp.float32))
-        values.append(tv[...])
+        scores.append(lax.dot_general(q, tk, contract, preferred_element_type=jnp.float32))
+        values.append(tv)
         highest = functools.reduce(
             jnp.maximum, [jnp.max(s, axis=1, keepdims=True) for s in scores]
         )
@@ -103,15 +98,28 @@
         o_ref[n * block : (n + 1) * block, :] = (out / total).astype(o_ref.dtype)
 
 
-def attend(q, own, left, right, text, head_dim, cols, part, parts):
+def window_bias(cols):
+    block = QROWS * cols
+    query = lax.broadcasted_iota(jnp.int32, (3, block, 3 * block), 1)
+    key = lax.broadcasted_iota(jnp.int32, (3, block, 3 * block), 2)
+    side = lax.broadcasted_iota(jnp.int32, (3, block, 3 * block), 0) - 1
+    row_gap = key // cols - QROWS - query // cols
+    col_gap = key % cols + side * cols - query % cols
+    near = (jnp.abs(row_gap) <= RADIUS) & (jnp.abs(col_gap) <= RADIUS)
+    return jnp.where(near, 0.0, -1e30).astype(jnp.float32)
+
+
+def attend(q, own, left, right, panel, text_rows, window, head_dim, cols, part, parts):
     rows, inner = q.shape
     block = QROWS * cols
     row_blocks = rows // block
     per = row_blocks // parts
     q_blocks = tuple(range(part * per, (part + 1) * per))
-    text_count = text[0].shape[0]
+    text_count = panel.shape[0] * text_rows // 2
+    text_at = panel.shape[1] // text_rows - 1
     whole = pl.BlockSpec((rows, head_dim), lambda h: (0, h))
-    texts = pl.BlockSpec((text_count, head_dim), lambda h: (0, h))
+    texts = pl.BlockSpec((panel.shape[0], text_rows, head_dim), lambda h: (0, text_at, h))
+    masks = pl.BlockSpec(window.shape, lambda h: (0, 0, 0), pipeline_mode=pl.Buffered(1))
     pairs = per * block * (9 * block + text_count)
     return pl.pallas_call(
         functools.partial(attn_kernel, q_blocks, row_blocks, cols),
@@ -119,16 +127,15 @@
         grid=(inner // head_dim,),
         in_specs=[pl.BlockSpec((per * block, head_dim), lambda h: (part, h))]
         + [whole] * 6
-        + [texts] * 2,
+        + [texts, masks],
         out_specs=pl.BlockSpec((per * block, head_dim), lambda h: (0, h)),
-        scratch_shapes=[pltpu.VMEM((3, block, 3 * block), jnp.float32)],
         compiler_params=pltpu.CompilerParams(vmem_limit_bytes=VMEM_LIMIT),
         cost_estimate=pl.CostEstimate(
             flops=4 * pairs * inner,
             bytes_accessed=2 * (6 * rows * inner + 2 * text_count * inner + 2 * per * block * inner),
             transcendentals=pairs * (inner // head_dim),
         ),
-    )(q, *own, *left, *right, *text)
+    )(q, *own, *left, *right, panel, window)
 
 
 def out_kernel(groups, me_ref, *refs):
@@ -212,8 +219,16 @@
     inner_here = qkv_weight.shape[2]
     flat_weight = qkv_weight.reshape(qkv_weight.shape[0], 3 * inner_here)
     gather_rows = functools.partial(lax.all_gather, axis_name="lon", axis=0, tiled=True)
-    k_rows = gather_rows(flat_weight[:, inner_here : 2 * inner_here])
-    v_rows = gather_rows(flat_weight[:, 2 * inner_here :])
+    kv_rows = gather_rows(flat_weight[:, inner_here:])
+    text_rows = 2 * text_kv.shape[1]
+    query_text = jnp.concatenate(
+        [flat_weight[:, :inner_here], text_kv.reshape(text_rows, inner_here)], axis=0
+    )
+    out_cols = model_width // head_groups
+    col_offset = lax.axis_index("head") * out_cols
+    own_image = lax.dynamic_slice_in_dim(
+        image_tokens.reshape(token_count, model_width), col_offset, out_cols, 1
+    )
     slice_rows = mod_weight.shape[0]
     row_offset = (lax.axis_index("lon") * head_groups + lax.axis_index("head")) * slice_rows
     silu_part = jax.nn.silu(
@@ -227,8 +242,10 @@
     modulation = lax.psum(partial_mod, ("lon", "head")).reshape(3, model_width) + mod_bias.astype(
         jnp.float32
     )
-    modulation, q_here = lax.optimization_barrier((modulation, flat_weight[:, :inner_here]))
-    q_rows = gather_rows(q_here)
+    modulation, query_text, own_image = lax.optimization_barrier(
+        (modulation, query_text, own_image)
+    )
+    panel = lax.all_gather(query_text, "lon", axis=0)
     token_values = image_tokens.reshape(token_count, model_width).astype(jnp.float32)
     average = jnp.mean(token_values, axis=1, keepdims=True)
     centred = token_values - average
@@ -239,10 +256,8 @@
     local_inner = qkv_weight.shape[2]
     head_dim = q_gain.shape[0]
     bias = qkv_bias.astype(jnp.float32)
-    own_k = project(modulated, k_rows, 0, bias[1], k_gain, True)
-    own_k, text_here = lax.optimization_barrier((own_k, text_kv))
-    text_panel = lax.all_gather(text_here, "lon", axis=1, tiled=True)
-    own_v = project(modulated, v_rows, 0, bias[2], k_gain, False)
+    own_k = project(modulated, kv_rows[None], 0, bias[1], k_gain, True)
+    own_v = project(modulated, kv_rows[None], local_inner, bias[2], k_gain, False)
     own_v, proj_here = lax.optimization_barrier((own_v, proj_weight))
     proj_columns = gather_rows(proj_here)
     count = lax.axis_size("lon")
@@ -250,21 +265,16 @@
     down = [((i + 1) % count, i) for i in range(count)]
     left = (lax.ppermute(own_k, "lon", up), lax.ppermute(own_v, "lon", up))
     right = (lax.ppermute(own_k, "lon", down), lax.ppermute(own_v, "lon", down))
-    queries = project(modulated, q_rows, 0, bias[0], q_gain, True)
-    out_cols = model_width // head_groups
-    col_offset = lax.axis_index("head") * out_cols
-    own_image = lax.dynamic_slice_in_dim(
-        image_tokens.reshape(token_count, model_width), col_offset, out_cols, 1
-    )
+    queries = project(modulated, panel, 0, bias[0], q_gain, True)
     own_gate = lax.dynamic_slice_in_dim(modulation[2], col_offset, out_cols, 0)
     own_bias = lax.dynamic_slice_in_dim(proj_bias, col_offset, out_cols, 0).astype(jnp.float32)
-    text = (text_panel[0], text_panel[1])
+    window = window_bias(col_count)
     parts = lat_rows // QROWS
     rows = token_count // parts
     blocks = []
     for part in range(parts):
         attended = attend(
-            queries, (own_k, own_v), left, right, text, head_dim, col_count, part, parts
+            queries, (own_k, own_v), left, right, panel, text_rows, window, head_dim, col_count, part, parts
         )
         blocks.append(exchange(attended))
     block_output = None

time: 344 us -> 345 us (level)
  waiting for transfers between devices: 126 us -> 119 us
  local copies, waits for them, and re-layouts: 16.6 us -> 22.5 us
  starting transfers between devices: 22.4 us -> 18.2 us
    all_gather x4 -> x2, waiting for transfers between devices: 117 us -> 99.3 us  [the longest x1 74.7 us: body(): panel = lax.all_gather(query_text, 'lon', axis=0)]
    all_gather x0 -> x1, local copies, waits for them, and re-layouts: none -> 8.63 us  [body(): panel = lax.all_gather(query_text, 'lon', axis=0)]
    ppermute x12, waiting for transfers between devices: 1.72 us -> 8.7 us  [exchange(): lax.ppermute(block, 'head', [(peer(i, k, groups), i) for i in range(group...]
    ppermute x2, waiting for transfers between devices: 0.01 us -> 5.96 us  [body(): right = (lax.ppermute(own_k, 'lon', down), lax.ppermute(own_v, 'lon', down))]
    unnamed x35 -> x36, local copies, waits for them, and re-layouts: 6.51 us -> 7.29 us
  transfers between devices with their start and end apart: 21 -> 19, of which waited for: 7 -> 7; matrix products, arithmetic and copies ran while one was open for 9% -> 11% of each run, Pallas kernels for 28% -> 28%
where the time goes in v4:
time: 345 us; the launch traced here: 342 us
  waiting for transfers between devices  119 us (34%)
  Pallas kernels  102 us (30%)
  blocking collectives  45.3 us (13%)
  local copies, waits for them, and re-layouts  22.5 us (7%)
  other arithmetic  20.6 us (6%)
  starting transfers between devices  18.2 us (5%)
  between operations  13.4 us (4%)
    all_gather x1, waiting for transfers between devices, body(): panel = lax.all_gather(query_text, 'lon', axis=0)  74.7 us
    psum x1, blocking collectives, body(): lax.psum(partial_mod, ('lon', 'head')).reshape(3, model_width)  45.3 us
    pallas_call x4, Pallas kernels, attend(): pl.pallas_call(functools.partial(attn_kernel, q_blocks, row_blocks, cols)...  44.6 us
    pallas_call x3, Pallas kernels, project(): pl.pallas_call(functools.partial(proj_kernel, normed, head_dim), out_shap...  36.7 us
    all_gather x1, waiting for transfers between devices, body(): kv_rows = gather_rows(flat_weight[:, inner_here:])  24.6 us
    pallas_call x4, Pallas kernels, output(): pl.pallas_call(functools.partial(out_kernel, groups), out_shape=jax.Shape...  20.4 us
    ppermute x12, starting transfers between devices, exchange(): lax.ppermute(block, 'head', [(peer(i, k, groups), i) for i in range(group...  14.2 us
    ppermute x12, waiting for transfers between devices, exchange(): lax.ppermute(block, 'head', [(peer(i, k, groups), i) for i in range(group...  8.7 us
  transfers between devices with their start and end apart: 19, of which 7 were waited for; matrix products, arithmetic and copies ran while one was open for 11% of the time, Pallas kernels for 28%

profile of v4, /device:TPU:0, one launch (start us, length us, event | category | flops | bytes accessed | tf_op | source)
XLA Modules:
  0.0 342.2 jit_solution(6789871835521135328)
XLA Ops:
  6.5 2.8 copy.22
  14.4 45.3 %psum.7 = f32[3,3072]{1,0:T(4,128)S(1)} all-reduce(f32[3,3072]{1,0:T(4,128)S(1)} %reshape.80), channel_id=1, replica_groups=mesh['lon'=8,'head'=4] {'lon','head'}, use_global_device_ids=true, to_apply=%region_0.1 | all-reduce | flops 9216 | bytes 73728 | tf_op jit(solution)/shard_map/psum | solution.py:242
  63.4 3.7 %convert_reduce_fusion = f32[64,16]{1,0:T(8,128)S(1)} fusion(bf16[64,16,3072]{2,1,0:T(8,128)(2,1)} %param.11), kind=kLoop, calls=%fused_computation.1 | loop fusion | flops 6290432 | bytes 6295552 | tf_op jit(solution)/shard_map/reduce_sum | solution.py:250
  67.2 4.7 %fusion.1 = f32[64,16]{1,0:T(8,128)S(1)} fusion(bf16[64,16,3072]{2,1,0:T(8,128)(2,1)} %param.11, f32[64,16]{1,0:T(8,128)S(1)} %broadcast_multiply_fusion), kind=kLoop, calls=%fused_computation.3 | loop fusion | flops 12581888 | bytes 6299648 | tf_op jit(solution)/shard_map/reduce_sum | solution.py:252
  72.7 8.2 %add_convert_fusion.x_ref = bf16[1024,3072]{1,0:T(8,128)(2,1)} fusion(f32[3072]{0:T(1024)S(1)} %bitcast.31, f32[1024]{0:T(1024)S(1)} %rsqrt.12, f32[1024]{0:T(1024)S(1)} %div.42, f32[3072]{0:T(1024)S(1)} %bitcast.32, bf16[64,16,3072]{2,1,0:T(8,128)(2,1)} %param.11), kind=kLoop, calls=%fused_computation.4 | loop fusion | flops 18874368 | bytes 12615680 | tf_op jit(solution)/shard_map/convert_element_type | solution.py:255
  80.9 24.6 %all-gather.5.cloned.1.call-done = bf16[3072,1536]{1,0:T(8,128)(2,1)} async-done(((bf16[384,1536]{1,0:T(8,128)(2,1)}), bf16[3072,1536]{1,0:T(8,128)(2,1)}) %all-gather.5.cloned.1.call-update) | async-done | bytes 9437200 | tf_op jit(solution)/shard_map/all_gather | solution.py:222
  105.5 11.5 %shard_map.111.vc = bf16[1024,768]{1,0:T(8,128)(2,1)} custom-call(bf16[1024,3072]{1,0:T(8,128)(2,1)} %add_convert_fusion.x_ref, bf16[1,3072,1536]{2,1,0:T(8,128)(2,1)} %bitcast.33, f32[1,768]{1,0:T(1,128)} %get-tuple-element.18.b_ref, f32[1,128]{1,0:T(1,128)} %bitcast.35), custom_call_target="tpu_custom_call" | custom-call | flops 4831838208 | bytes 12582912 | tf_op jit(solution)/shard_map/pallas_call | solution.py:43
  117.6 12.6 %shard_map.110.kc = bf16[1024,768]{1,0:T(8,128)(2,1)} custom-call(bf16[1024,3072]{1,0:T(8,128)(2,1)} %add_convert_fusion.x_ref, bf16[1,3072,1536]{2,1,0:T(8,128)(2,1)} %bitcast.34, f32[1,768]{1,0:T(1,128)} %get-tuple-element.19.b_ref, f32[1,128]{1,0:T(1,128)} %bitcast.36), custom_call_target="tpu_custom_call" | custom-call | flops 4831838208 | bytes 12582912 | tf_op jit(solution)/shard_map/pallas_call | solution.py:43
  130.2 3.4 collective-permute-start.2
  135.8 74.7 %all-gather.9.cloned.1.call-done = bf16[4096,768]{0,1:T(8,128)(2,1)} async-done(((bf16[512,768]{0,1:T(8,128)(2,1)}), bf16[4096,768]{0,1:T(8,128)(2,1)}) %all-gather.9.cloned.1.call-update) | async-done | bytes 6291472 | tf_op jit(solution)/shard_map/all_gather | solution.py:248
  210.5 8.6 %copy.24 = bf16[4096,768]{1,0:T(8,128)(2,1)} copy(bf16[4096,768]{0,1:T(8,128)(2,1)} %all-gather.9.cloned.1.call-done) | data formatting | bytes 12582912 | tf_op jit(solution)/shard_map/all_gather | solution.py:248
  219.1 12.6 %shard_map.109.q_ref = bf16[1024,768]{1,0:T(8,128)(2,1)} custom-call(bf16[1024,3072]{1,0:T(8,128)(2,1)} %add_convert_fusion.x_ref, bf16[8,512,768]{2,1,0:T(8,128)(2,1)} %bitcast.19, f32[1,768]{1,0:T(1,128)} %get-tuple-element.20.b_ref, f32[1,128]{1,0:T(1,128)} %bitcast.37), custom_call_target="tpu_custom_call" | custom-call | flops 4831838208 | bytes 12582912 | tf_op jit(solution)/shard_map/pallas_call | solution.py:43
  231.7 6.0 %collective-permute-done.2.kr = bf16[1024,768]{1,0:T(8,128)(2,1)} collective-permute-done((bf16[1024,768]{1,0:T(8,128)(2,1)}, bf16[1024,768]{1,0:T(8,128)(2,1)}, u32[]{:S(2)}, u32[]{:S(2)}) %collective-permute-start.2) | collective-permute-done | bytes 1572896 | tf_op jit(solution)/shard_map/ppermute | solution.py:267
  237.7 5.1 %collective-permute-done.kl = bf16[1024,768]{1,0:T(8,128)(2,1)} collective-permute-done((bf16[1024,768]{1,0:T(8,128)(2,1)}, bf16[1024,768]{1,0:T(8,128)(2,1)}, u32[]{:S(2)}, u32[]{:S(2)}) %collective-permute-start) | collective-permute-done | bytes 1572896 | tf_op jit(solution)/shard_map/ppermute | solution.py:266
  242.8 11.9 %shard_map.113.refs_0_ = bf16[256,768]{1,0:T(8,128)(2,1)} custom-call(bf16[1024,768]{1,0:T(8,128)(2,1)} %shard_map.109.q_ref, bf16[1024,768]{1,0:T(8,128)(2,1)} %shard_map.110.kc, bf16[1024,768]{1,0:T(8,128)(2,1)} %shard_map.111.vc, bf16[1024,768]{1,0:T(8,128)(2,1)} %collective-permute-done.kl, bf16[1024,768]{1,0:T(8,128)(2,1)} %copy-done.1, ...), custom_call_target="tpu_custom_call" | custom-call | flops 2214592512 | bytes 11796480 | tf_op jit(solution)/shard_map/pallas_call | solution.py:124
  257.1 11.9 %shard_map.114.refs_0_ = bf16[256,768]{1,0:T(8,128)(2,1)} custom-call(bf16[1024,768]{1,0:T(8,128)(2,1)} %shard_map.109.q_ref, bf16[1024,768]{1,0:T(8,128)(2,1)} %shard_map.110.kc, bf16[1024,768]{1,0:T(8,128)(2,1)} %shard_map.111.vc, bf16[1024,768]{1,0:T(8,128)(2,1)} %collective-permute-done.kl, bf16[1024,768]{1,0:T(8,128)(2,1)} %copy-done.1, ...), custom_call_target="tpu_custom_call" | custom-call | flops 2214592512 | bytes 11796480 | tf_op jit(solution)/shard_map/pallas_call | solution.py:124
  272.6 10.4 %shard_map.115.refs_0_ = bf16[256,768]{1,0:T(8,128)(2,1)} custom-call(bf16[1024,768]{1,0:T(8,128)(2,1)} %shard_map.109.q_ref, bf16[1024,768]{1,0:T(8,128)(2,1)} %shard_map.110.kc, bf16[1024,768]{1,0:T(8,128)(2,1)} %shard_map.111.vc, bf16[1024,768]{1,0:T(8,128)(2,1)} %collective-permute-done.kl, bf16[1024,768]{1,0:T(8,128)(2,1)} %copy-done.1, ...), custom_call_target="tpu_custom_call" | custom-call | flops 2214592512 | bytes 11796480 | tf_op jit(solution)/shard_map/pallas_call | solution.py:124
  287.2 3.5 %collective-permute-done.11.refs_2_ = bf16[256,768]{1,0:T(8,128)(2,1)S(1)} collective-permute-done((bf16[256,768]{1,0:T(8,128)(2,1)}, bf16[256,768]{1,0:T(8,128)(2,1)S(1)}, u32[]{:S(2)}, u32[]{:S(2)}) %collective-permute-start.11) | collective-permute-done | bytes 393248 | tf_op jit(solution)/shard_map/ppermute | solution.py:164
  291.8 10.4 %shard_map.112.refs_0_ = bf16[256,768]{1,0:T(8,128)(2,1)} custom-call(bf16[1024,768]{1,0:T(8,128)(2,1)} %shard_map.109.q_ref, bf16[1024,768]{1,0:T(8,128)(2,1)} %shard_map.110.kc, bf16[1024,768]{1,0:T(8,128)(2,1)} %shard_map.111.vc, bf16[1024,768]{1,0:T(8,128)(2,1)} %collective-permute-done.kl, bf16[1024,768]{1,0:T(8,128)(2,1)} %copy-done.1, ...), custom_call_target="tpu_custom_call" | custom-call | flops 2214592512 | bytes 11796480 | tf_op jit(solution)/shard_map/pallas_call | solution.py:124
  308.4 5.1 %shard_map.116.refs_8_ = bf16[1024,768]{1,0:T(8,128)(2,1)} custom-call(s32[1]{0:T(128)} %bitcast.me_ref, bf16[256,768]{1,0:T(8,128)(2,1)} %shard_map.115.refs_0_, bf16[256,768]{1,0:T(8,128)(2,1)} %collective-permute-done.13.refs_1_, bf16[256,768]{1,0:T(8,128)(2,1)} %copy-done.9, bf16[256,768]{1,0:T(8,128)(2,1)} %copy-done.7, ...), custom_call_target="tpu_custom_call" | custom-call | flops 1207959552 | bytes 7077888 | tf_op jit(solution)/shard_map/pallas_call | solution.py:187
  313.5 5.1 %shard_map.117.refs_8_ = bf16[1024,768]{1,0:T(8,128)(2,1)} custom-call(s32[1]{0:T(128)} %bitcast.me_ref, bf16[256,768]{1,0:T(8,128)(2,1)} %shard_map.114.refs_0_, bf16[256,768]{1,0:T(8,128)(2,1)} %copy-done.6, bf16[256,768]{1,0:T(8,128)(2,1)} %copy-done.5, bf16[256,768]{1,0:T(8,128)(2,1)} %copy-done.4, ...), custom_call_target="tpu_custom_call", output_to_operand_aliasing={{}: (9, {})} | custom-call | flops 1207959552 | bytes 7077888 | tf_op jit(solution)/shard_map/pallas_call | solution.py:187
  320.2 5.1 %shard_map.118.refs_8_ = bf16[1024,768]{1,0:T(8,128)(2,1)} custom-call(s32[1]{0:T(128)} %bitcast.me_ref, bf16[256,768]{1,0:T(8,128)(2,1)} %shard_map.113.refs_0_, bf16[256,768]{1,0:T(8,128)(2,1)} %copy-done.10, bf16[256,768]{1,0:T(8,128)(2,1)} %copy-done.8, bf16[256,768]{1,0:T(8,128)(2,1)} %copy-done.3, ...), custom_call_target="tpu_custom_call", output_to_operand_aliasing={{}: (9, {})} | custom-call | flops 1207959552 | bytes 7077888 | tf_op jit(solution)/shard_map/pallas_call | solution.py:187
  325.3 3.8 %collective-permute-done.5.refs_2_ = bf16[256,768]{1,0:T(8,128)(2,1)S(1)} collective-permute-done((bf16[256,768]{1,0:T(8,128)(2,1)}, bf16[256,768]{1,0:T(8,128)(2,1)S(1)}, u32[]{:S(2)}, u32[]{:S(2)}) %collective-permute-start.5) | collective-permute-done | bytes 393248 | tf_op jit(solution)/shard_map/ppermute | solution.py:164
  330.6 5.1 %shard_map.119 = bf16[1024,768]{1,0:T(8,128)(2,1)} custom-call(s32[1]{0:T(128)} %bitcast.me_ref, bf16[256,768]{1,0:T(8,128)(2,1)} %shard_map.112.refs_0_, bf16[256,768]{1,0:T(8,128)(2,1)} %copy-done.13, bf16[256,768]{1,0:T(8,128)(2,1)} %copy-done.12, bf16[256,768]{1,0:T(8,128)(2,1)} %copy-done.11, ...), custom_call_target="tpu_custom_call", output_to_operand_aliasing={{}: (9, {})} | custom-call | flops 1207959552 | bytes 7077888 | tf_op jit(solution)/shard_map/pallas_call | solution.py:187
  (95 shorter events, 32.9 us)
Async XLA Ops:
  6.5 99.0 %all-gather.5.cloned.1.call-start = ((), (), s32[]{:S(2)}) async-start(), calls=%async_computation | async-start | bytes 10616832 | tf_op jit(solution)/shard_map/all_gather | solution.py:222
  10.9 199.6 %all-gather.9.cloned.1.call-start = ((), (), s32[]{:S(2)}) async-start(), calls=%async_computation.2 | async-start | bytes 7077888 | tf_op jit(solution)/shard_map/all_gather | solution.py:248
  63.4 245.0 %all-gather.7.cloned.1.call-start = ((), (), s32[]{:S(2)}) async-start(), calls=%async_computation.1 | async-start | bytes 5308416 | tf_op jit(solution)/shard_map/all_gather | solution.py:262
  117.0 114.7 %collective-permute-start.3 = (bf16[1024,768]{1,0:T(8,128)(2,1)}, bf16[1024,768]{1,0:T(8,128)(2,1)S(1)}, u32[]{:S(2)}, u32[]{:S(2)}) collective-permute-start(bf16[1024,768]{1,0:T(8,128)(2,1)} %shard_map.111.vc), channel_id=1, source_target_pairs={{4,0},{8,4},{12,8},{16,12},{20,16},{24,20},{28,24},{0,28},{5,1},{9... | collective-permute-start | bytes 4718600 | tf_op jit(solution)/shard_map/ppermute | solution.py:267
  117.4 114.3 %collective-permute-start.1 = (bf16[1024,768]{1,0:T(8,128)(2,1)}, bf16[1024,768]{1,0:T(8,128)(2,1)S(1)}, u32[]{:S(2)}, u32[]{:S(2)}) collective-permute-start(bf16[1024,768]{1,0:T(8,128)(2,1)} %shard_map.111.vc), channel_id=1, source_target_pairs={{0,4},{4,8},{8,12},{12,16},{16,20},{20,24},{24,28},{28,0},{1,5},{5... | collective-permute-start | bytes 4718600 | tf_op jit(solution)/shard_map/ppermute | solution.py:266
  130.2 107.5 %collective-permute-start.2 = (bf16[1024,768]{1,0:T(8,128)(2,1)}, bf16[1024,768]{1,0:T(8,128)(2,1)}, u32[]{:S(2)}, u32[]{:S(2)}) collective-permute-start(bf16[1024,768]{1,0:T(8,128)(2,1)} %shard_map.110.kc), channel_id=1, source_target_pairs={{4,0},{8,4},{12,8},{16,12},{20,16},{24,20},{28,24},{0,28},{5,1},{9... | collective-permute-start | bytes 4718600 | tf_op jit(solution)/shard_map/ppermute | solution.py:267
  133.6 109.2 %collective-permute-start = (bf16[1024,768]{1,0:T(8,128)(2,1)}, bf16[1024,768]{1,0:T(8,128)(2,1)}, u32[]{:S(2)}, u32[]{:S(2)}) collective-permute-start(bf16[1024,768]{1,0:T(8,128)(2,1)} %shard_map.110.kc), channel_id=1, source_target_pairs={{0,4},{4,8},{8,12},{12,16},{16,20},{20,24},{24,28},{28,0},{1,5},{5... | collective-permute-start | bytes 4718600 | tf_op jit(solution)/shard_map/ppermute | solution.py:266
  231.7 11.1 %copy-start = (bf16[1024,768]{1,0:T(8,128)(2,1)}, bf16[1024,768]{1,0:T(8,128)(2,1)S(1)}, u32[]{:S(2)}) copy-start(bf16[1024,768]{1,0:T(8,128)(2,1)S(1)} %collective-permute-done.3.vr) | copy-start | bytes 4718596
  254.7 28.8 %collective-permute-start.9 = (bf16[256,768]{1,0:T(8,128)(2,1)}, bf16[256,768]{1,0:T(8,128)(2,1)S(1)}, u32[]{:S(2)}, u32[]{:S(2)}) collective-permute-start(bf16[256,768]{1,0:T(8,128)(2,1)} %shard_map.113.refs_0_), channel_id=1, source_target_pairs={{3,0},{2,1},{1,2},{0,3},{7,4},{6,5},{5,6},{4,7},{11,8},{10,9},{9,1... | collective-permute-start | bytes 1179656 | tf_op jit(solution)/shard_map/ppermute | solution.py:164
  269.0 21.7 %copy-start.2 = (bf16[256,768]{1,0:T(8,128)(2,1)S(1)}, bf16[256,768]{1,0:T(8,128)(2,1)}, u32[]{:S(2)}) copy-start(bf16[256,768]{1,0:T(8,128)(2,1)} %shard_map.113.refs_0_) | copy-start | bytes 1179652
  269.0 16.0 %collective-permute-start.12 = (bf16[256,768]{1,0:T(8,128)(2,1)}, bf16[256,768]{1,0:T(8,128)(2,1)S(1)}, u32[]{:S(2)}, u32[]{:S(2)}) collective-permute-start(bf16[256,768]{1,0:T(8,128)(2,1)} %shard_map.114.refs_0_), channel_id=1, source_target_pairs={{3,0},{2,1},{1,2},{0,3},{7,4},{6,5},{5,6},{4,7},{11,8},{10,9},{9,1... | collective-permute-start | bytes 1179656 | tf_op jit(solution)/shard_map/ppermute | solution.py:164
  269.6 21.1 %collective-permute-start.11 = (bf16[256,768]{1,0:T(8,128)(2,1)}, bf16[256,768]{1,0:T(8,128)(2,1)S(1)}, u32[]{:S(2)}, u32[]{:S(2)}) collective-permute-start(bf16[256,768]{1,0:T(8,128)(2,1)} %shard_map.114.refs_0_), channel_id=1, source_target_pairs={{2,0},{3,1},{0,2},{1,3},{6,4},{7,5},{4,6},{5,7},{10,8},{11,9},{8,1... | collective-permute-start | bytes 1179656 | tf_op jit(solution)/shard_map/ppermute | solution.py:164
  271.2 20.2 %collective-permute-start.10 = (bf16[256,768]{1,0:T(8,128)(2,1)}, bf16[256,768]{1,0:T(8,128)(2,1)S(1)}, u32[]{:S(2)}, u32[]{:S(2)}) collective-permute-start(bf16[256,768]{1,0:T(8,128)(2,1)} %shard_map.114.refs_0_), channel_id=1, source_target_pairs={{1,0},{0,1},{3,2},{2,3},{5,4},{4,5},{7,6},{6,7},{9,8},{8,9},{11,10... | collective-permute-start | bytes 1179656 | tf_op jit(solution)/shard_map/ppermute | solution.py:164
  282.9 19.3 %collective-permute-start.15 = (bf16[256,768]{1,0:T(8,128)(2,1)}, bf16[256,768]{1,0:T(8,128)(2,1)S(1)}, u32[]{:S(2)}, u32[]{:S(2)}) collective-permute-start(bf16[256,768]{1,0:T(8,128)(2,1)} %shard_map.115.refs_0_), channel_id=1, source_target_pairs={{3,0},{2,1},{1,2},{0,3},{7,4},{6,5},{5,6},{4,7},{11,8},{10,9},{9,1... | collective-permute-start | bytes 1179656 | tf_op jit(solution)/shard_map/ppermute | solution.py:164
  283.5 18.7 %copy-start.3 = (bf16[256,768]{1,0:T(8,128)(2,1)}, bf16[256,768]{1,0:T(8,128)(2,1)S(1)}, u32[]{:S(2)}) copy-start(bf16[256,768]{1,0:T(8,128)(2,1)S(1)} %collective-permute-done.9.refs_3_) | copy-start | bytes 1179652
  283.5 21.2 %collective-permute-start.14 = (bf16[256,768]{1,0:T(8,128)(2,1)}, bf16[256,768]{1,0:T(8,128)(2,1)S(1)}, u32[]{:S(2)}, u32[]{:S(2)}) collective-permute-start(bf16[256,768]{1,0:T(8,128)(2,1)} %shard_map.115.refs_0_), channel_id=1, source_target_pairs={{2,0},{3,1},{0,2},{1,3},{6,4},{7,5},{4,6},{5,7},{10,8},{11,9},{8,1... | collective-permute-start | bytes 1179656 | tf_op jit(solution)/shard_map/ppermute | solution.py:164
  285.0 17.2 %copy-start.4 = (bf16[256,768]{1,0:T(8,128)(2,1)}, bf16[256,768]{1,0:T(8,128)(2,1)S(1)}, u32[]{:S(2)}) copy-start(bf16[256,768]{1,0:T(8,128)(2,1)S(1)} %collective-permute-done.12.refs_3_) | copy-start | bytes 1179652
  285.0 21.7 %collective-permute-start.13 = (bf16[256,768]{1,0:T(8,128)(2,1)}, bf16[256,768]{1,0:T(8,128)(2,1)}, u32[]{:S(2)}, u32[]{:S(2)}) collective-permute-start(bf16[256,768]{1,0:T(8,128)(2,1)} %shard_map.115.refs_0_), channel_id=1, source_target_pairs={{1,0},{0,1},{3,2},{2,3},{5,4},{4,5},{7,6},{6,7},{9,8},{8,9},{11,10... | collective-permute-start | bytes 1179656 | tf_op jit(solution)/shard_map/ppermute | solution.py:164
  290.7 11.5 %copy-start.5 = (bf16[256,768]{1,0:T(8,128)(2,1)}, bf16[256,768]{1,0:T(8,128)(2,1)S(1)}, u32[]{:S(2)}) copy-start(bf16[256,768]{1,0:T(8,128)(2,1)S(1)} %collective-permute-done.11.refs_2_) | copy-start | bytes 1179652
  290.7 27.9 %collective-permute-start.8 = (bf16[256,768]{1,0:T(8,128)(2,1)S(1)}, bf16[256,768]{1,0:T(8,128)(2,1)S(1)}, u32[]{:S(2)}, u32[]{:S(2)}) collective-permute-start(bf16[256,768]{1,0:T(8,128)(2,1)S(1)} %copy-done.2), channel_id=1, source_target_pairs={{2,0},{3,1},{0,2},{1,3},{6,4},{7,5},{4,6},{5,7},{10,8},{11,9},{8,1... | collective-permute-start | bytes 1179656 | tf_op jit(solution)/shard_map/ppermute | solution.py:164
  291.4 27.3 %collective-permute-start.7 = (bf16[256,768]{1,0:T(8,128)(2,1)S(1)}, bf16[256,768]{1,0:T(8,128)(2,1)S(1)}, u32[]{:S(2)}, u32[]{:S(2)}) collective-permute-start(bf16[256,768]{1,0:T(8,128)(2,1)S(1)} %copy-done.2), channel_id=1, source_target_pairs={{1,0},{0,1},{3,2},{2,3},{5,4},{4,5},{7,6},{6,7},{9,8},{8,9},{11,10... | collective-permute-start | bytes 1179656 | tf_op jit(solution)/shard_map/ppermute | solution.py:164
  302.3 23.0 %collective-permute-start.6 = (bf16[256,768]{1,0:T(8,128)(2,1)}, bf16[256,768]{1,0:T(8,128)(2,1)S(1)}, u32[]{:S(2)}, u32[]{:S(2)}) collective-permute-start(bf16[256,768]{1,0:T(8,128)(2,1)} %shard_map.112.refs_0_), channel_id=1, source_target_pairs={{3,0},{2,1},{1,2},{0,3},{7,4},{6,5},{5,6},{4,7},{11,8},{10,9},{9,1... | collective-permute-start | bytes 1179656 | tf_op jit(solution)/shard_map/ppermute | solution.py:164
  304.7 24.3 %collective-permute-start.5 = (bf16[256,768]{1,0:T(8,128)(2,1)}, bf16[256,768]{1,0:T(8,128)(2,1)S(1)}, u32[]{:S(2)}, u32[]{:S(2)}) collective-permute-start(bf16[256,768]{1,0:T(8,128)(2,1)} %shard_map.112.refs_0_), channel_id=1, source_target_pairs={{2,0},{3,1},{0,2},{1,3},{6,4},{7,5},{4,6},{5,7},{10,8},{11,9},{8,1... | collective-permute-start | bytes 1179656 | tf_op jit(solution)/shard_map/ppermute | solution.py:164
  306.8 22.2 %collective-permute-start.4 = (bf16[256,768]{1,0:T(8,128)(2,1)}, bf16[256,768]{1,0:T(8,128)(2,1)S(1)}, u32[]{:S(2)}, u32[]{:S(2)}) collective-permute-start(bf16[256,768]{1,0:T(8,128)(2,1)} %shard_map.112.refs_0_), channel_id=1, source_target_pairs={{1,0},{0,1},{3,2},{2,3},{5,4},{4,5},{7,6},{6,7},{9,8},{8,9},{11,10... | collective-permute-start | bytes 1179656 | tf_op jit(solution)/shard_map/ppermute | solution.py:164
  (12 other events, 48.6 us)
Sparse Core Ops, SparseCore 0:
  11.0 94.4 all-gather.4
  107.1 103.3 all-gather.8
  212.2 63.2 all-gather.6

commit v5 on v4

--- a/solution.py
+++ b/solution.py
@@ -269,7 +269,7 @@
     own_gate = lax.dynamic_slice_in_dim(modulation[2], col_offset, out_cols, 0)
     own_bias = lax.dynamic_slice_in_dim(proj_bias, col_offset, out_cols, 0).astype(jnp.float32)
     window = window_bias(col_count)
-    parts = lat_rows // QROWS
+    parts = max(1, lat_rows // (2 * QROWS))
     rows = token_count // parts
     blocks = []
     for part in range(parts):

time: 345 us -> 345 us (level)
  waiting for transfers between devices: 119 us -> 147 us
  Pallas kernels: 102 us -> 83 us
  starting transfers between devices: 18.2 us -> 11.1 us
    ppermute x12 -> x6, waiting for transfers between devices: 8.7 us -> 36.3 us  [exchange(): lax.ppermute(block, 'head', [(peer(i, k, groups), i) for i in range(group...]
    pallas_call x4 -> x2, Pallas kernels: 44.6 us -> 32.6 us  [attend(): pl.pallas_call(functools.partial(attn_kernel, q_blocks, row_blocks, cols)...]
    ppermute x12 -> x6, starting transfers between devices: 14.2 us -> 7.11 us  [exchange(): lax.ppermute(block, 'head', [(peer(i, k, groups), i) for i in range(group...]
    pallas_call x4 -> x2, Pallas kernels: 20.4 us -> 13.7 us  [output(): pl.pallas_call(functools.partial(out_kernel, groups), out_shape=jax.Shape...]
    unnamed x36 -> x20, local copies, waits for them, and re-layouts: 7.29 us -> 5.33 us
  transfers between devices with their start and end apart: 19 -> 13, of which waited for: 7 -> 7; matrix products, arithmetic and copies ran while one was open for 11% -> 11% of each run, Pallas kernels for 28% -> 22%
where the time goes in v5:
time: 345 us; the launch traced here: 342 us
  waiting for transfers between devices  147 us (43%)
  Pallas kernels  83 us (24%)
  blocking collectives  45.3 us (13%)
  local copies, waits for them, and re-layouts  20.6 us (6%)
  other arithmetic  20.6 us (6%)
  between operations  13.3 us (4%)
  starting transfers between devices  11.1 us (3%)
    all_gather x1, waiting for transfers between devices, body(): panel = lax.all_gather(query_text, 'lon', axis=0)  74.7 us
    psum x1, blocking collectives, body(): lax.psum(partial_mod, ('lon', 'head')).reshape(3, model_width)  45.3 us
    pallas_call x3, Pallas kernels, project(): pl.pallas_call(functools.partial(proj_kernel, normed, head_dim), out_shap...  36.7 us
    ppermute x6, waiting for transfers between devices, exchange(): lax.ppermute(block, 'head', [(peer(i, k, groups), i) for i in range(group...  36.3 us
    pallas_call x2, Pallas kernels, attend(): pl.pallas_call(functools.partial(attn_kernel, q_blocks, row_blocks, cols)...  32.6 us
    all_gather x1, waiting for transfers between devices, body(): kv_rows = gather_rows(flat_weight[:, inner_here:])  24.5 us
    pallas_call x2, Pallas kernels, output(): pl.pallas_call(functools.partial(out_kernel, groups), out_shape=jax.Shape...  13.7 us
    all_gather x1, local copies, waits for them, and re-layouts, body(): panel = lax.all_gather(query_text, 'lon', axis=0)  8.64 us
  transfers between devices with their start and end apart: 13, of which 7 were waited for; matrix products, arithmetic and copies ran while one was open for 11% of the time, Pallas kernels for 22%

profile of v5, /device:TPU:0, one launch (start us, length us, event | category | flops | bytes accessed | tf_op | source)
XLA Modules:
  0.0 342.0 jit_solution(7933399375310445072)
XLA Ops:
  6.5 2.8 copy.20
  14.4 45.3 %psum.7 = f32[3,3072]{1,0:T(4,128)S(1)} all-reduce(f32[3,3072]{1,0:T(4,128)S(1)} %reshape.74), channel_id=1, replica_groups=mesh['lon'=8,'head'=4] {'lon','head'}, use_global_device_ids=true, to_apply=%region_0.1 | all-reduce | flops 9216 | bytes 73728 | tf_op jit(solution)/shard_map/psum | solution.py:242
  60.7 2.7 constant_dynamic-slice_fusion.1.refs_5_
  63.5 3.7 %convert_reduce_fusion = f32[64,16]{1,0:T(8,128)S(1)} fusion(bf16[64,16,3072]{2,1,0:T(8,128)(2,1)} %param.11), kind=kLoop, calls=%fused_computation.1 | loop fusion | flops 6290432 | bytes 6295552 | tf_op jit(solution)/shard_map/reduce_sum | solution.py:250
  67.3 4.7 %fusion.1 = f32[64,16]{1,0:T(8,128)S(1)} fusion(bf16[64,16,3072]{2,1,0:T(8,128)(2,1)} %param.11, f32[64,16]{1,0:T(8,128)S(1)} %broadcast_multiply_fusion), kind=kLoop, calls=%fused_computation.3 | loop fusion | flops 12581888 | bytes 6299648 | tf_op jit(solution)/shard_map/reduce_sum | solution.py:252
  72.7 8.3 %add_convert_fusion.x_ref = bf16[1024,3072]{1,0:T(8,128)(2,1)} fusion(f32[3072]{0:T(1024)S(1)} %bitcast.29, f32[1024]{0:T(1024)S(1)} %rsqrt.12, f32[1024]{0:T(1024)S(1)} %div.34, f32[3072]{0:T(1024)S(1)} %bitcast.30, bf16[64,16,3072]{2,1,0:T(8,128)(2,1)} %param.11), kind=kLoop, calls=%fused_computation.4 | loop fusion | flops 18874368 | bytes 12615680 | tf_op jit(solution)/shard_map/convert_element_type | solution.py:255
  81.0 24.5 %all-gather.5.cloned.1.call-done = bf16[3072,1536]{1,0:T(8,128)(2,1)} async-done(((bf16[384,1536]{1,0:T(8,128)(2,1)}), bf16[3072,1536]{1,0:T(8,128)(2,1)}) %all-gather.5.cloned.1.call-update) | async-done | bytes 9437200 | tf_op jit(solution)/shard_map/all_gather | solution.py:222
  105.5 11.5 %shard_map.111.vc = bf16[1024,768]{1,0:T(8,128)(2,1)} custom-call(bf16[1024,3072]{1,0:T(8,128)(2,1)} %add_convert_fusion.x_ref, bf16[1,3072,1536]{2,1,0:T(8,128)(2,1)} %bitcast.31, f32[1,768]{1,0:T(1,128)} %get-tuple-element.18.b_ref, f32[1,128]{1,0:T(1,128)} %bitcast.33), custom_call_target="tpu_custom_call" | custom-call | flops 4831838208 | bytes 12582912 | tf_op jit(solution)/shard_map/pallas_call | solution.py:43
  117.6 12.7 %shard_map.110.kc = bf16[1024,768]{1,0:T(8,128)(2,1)} custom-call(bf16[1024,3072]{1,0:T(8,128)(2,1)} %add_convert_fusion.x_ref, bf16[1,3072,1536]{2,1,0:T(8,128)(2,1)} %bitcast.32, f32[1,768]{1,0:T(1,128)} %get-tuple-element.19.b_ref, f32[1,128]{1,0:T(1,128)} %bitcast.34), custom_call_target="tpu_custom_call" | custom-call | flops 4831838208 | bytes 12582912 | tf_op jit(solution)/shard_map/pallas_call | solution.py:43
  130.2 3.4 collective-permute-start.2
  135.8 74.7 %all-gather.9.cloned.1.call-done = bf16[4096,768]{0,1:T(8,128)(2,1)} async-done(((bf16[512,768]{0,1:T(8,128)(2,1)}), bf16[4096,768]{0,1:T(8,128)(2,1)}) %all-gather.9.cloned.1.call-update) | async-done | bytes 6291472 | tf_op jit(solution)/shard_map/all_gather | solution.py:248
  210.5 8.6 %copy.22 = bf16[4096,768]{1,0:T(8,128)(2,1)} copy(bf16[4096,768]{0,1:T(8,128)(2,1)} %all-gather.9.cloned.1.call-done) | data formatting | bytes 12582912 | tf_op jit(solution)/shard_map/all_gather | solution.py:248
  219.1 12.6 %shard_map.109.q_ref = bf16[1024,768]{1,0:T(8,128)(2,1)} custom-call(bf16[1024,3072]{1,0:T(8,128)(2,1)} %add_convert_fusion.x_ref, bf16[8,512,768]{2,1,0:T(8,128)(2,1)} %bitcast.20, f32[1,768]{1,0:T(1,128)} %get-tuple-element.20.b_ref, f32[1,128]{1,0:T(1,128)} %bitcast.35), custom_call_target="tpu_custom_call" | custom-call | flops 4831838208 | bytes 12582912 | tf_op jit(solution)/shard_map/pallas_call | solution.py:43
  231.7 6.0 %collective-permute-done.2.kr = bf16[1024,768]{1,0:T(8,128)(2,1)} collective-permute-done((bf16[1024,768]{1,0:T(8,128)(2,1)}, bf16[1024,768]{1,0:T(8,128)(2,1)}, u32[]{:S(2)}, u32[]{:S(2)}) %collective-permute-start.2) | collective-permute-done | bytes 1572896 | tf_op jit(solution)/shard_map/ppermute | solution.py:267
  237.7 5.1 %collective-permute-done.kl = bf16[1024,768]{1,0:T(8,128)(2,1)} collective-permute-done((bf16[1024,768]{1,0:T(8,128)(2,1)}, bf16[1024,768]{1,0:T(8,128)(2,1)}, u32[]{:S(2)}, u32[]{:S(2)}) %collective-permute-start) | collective-permute-done | bytes 1572896 | tf_op jit(solution)/shard_map/ppermute | solution.py:266
  242.8 16.6 %shard_map.113.refs_0_ = bf16[512,768]{1,0:T(8,128)(2,1)} custom-call(bf16[1024,768]{1,0:T(8,128)(2,1)} %shard_map.109.q_ref, bf16[1024,768]{1,0:T(8,128)(2,1)} %shard_map.110.kc, bf16[1024,768]{1,0:T(8,128)(2,1)} %shard_map.111.vc, bf16[1024,768]{1,0:T(8,128)(2,1)} %collective-permute-done.kl, bf16[1024,768]{1,0:T(8,128)(2,1)} %copy-done.1, ...), custom_call_target="tpu_custom_call" | custom-call | flops 4429185024 | bytes 12582912 | tf_op jit(solution)/shard_map/pallas_call | solution.py:124
  259.3 2.5 collective-permute-start.9
  262.8 16.1 %shard_map.112.refs_0_ = bf16[512,768]{1,0:T(8,128)(2,1)} custom-call(bf16[1024,768]{1,0:T(8,128)(2,1)} %shard_map.109.q_ref, bf16[1024,768]{1,0:T(8,128)(2,1)} %shard_map.110.kc, bf16[1024,768]{1,0:T(8,128)(2,1)} %shard_map.111.vc, bf16[1024,768]{1,0:T(8,128)(2,1)} %collective-permute-done.kl, bf16[1024,768]{1,0:T(8,128)(2,1)} %copy-done.1, ...), custom_call_target="tpu_custom_call" | custom-call | flops 4429185024 | bytes 12582912 | tf_op jit(solution)/shard_map/pallas_call | solution.py:124
  278.9 2.5 collective-permute-start.6
  284.4 13.4 %collective-permute-done.8.refs_2_ = bf16[512,768]{1,0:T(8,128)(2,1)S(1)} collective-permute-done((bf16[512,768]{1,0:T(8,128)(2,1)}, bf16[512,768]{1,0:T(8,128)(2,1)S(1)}, u32[]{:S(2)}, u32[]{:S(2)}) %collective-permute-start.8) | collective-permute-done | bytes 786464 | tf_op jit(solution)/shard_map/ppermute | solution.py:164
  299.0 6.8 %shard_map.114.refs_8_ = bf16[1024,768]{1,0:T(8,128)(2,1)} custom-call(s32[1]{0:T(128)} %bitcast.me_ref, bf16[512,768]{1,0:T(8,128)(2,1)} %shard_map.113.refs_0_, bf16[512,768]{1,0:T(8,128)(2,1)} %copy-done.5, bf16[512,768]{1,0:T(8,128)(2,1)} %copy-done.3, bf16[512,768]{1,0:T(8,128)(2,1)} %copy-done.2, ...), custom_call_target="tpu_custom_call" | custom-call | flops 2415919104 | bytes 9437184 | tf_op jit(solution)/shard_map/pallas_call | solution.py:187
  305.8 8.9 %collective-permute-done.6.refs_3_ = bf16[512,768]{1,0:T(8,128)(2,1)S(1)} collective-permute-done((bf16[512,768]{1,0:T(8,128)(2,1)}, bf16[512,768]{1,0:T(8,128)(2,1)S(1)}, u32[]{:S(2)}, u32[]{:S(2)}) %collective-permute-start.6) | collective-permute-done | bytes 786464 | tf_op jit(solution)/shard_map/ppermute | solution.py:164
  314.7 14.0 %collective-permute-done.5.refs_2_ = bf16[512,768]{1,0:T(8,128)(2,1)} collective-permute-done((bf16[512,768]{1,0:T(8,128)(2,1)}, bf16[512,768]{1,0:T(8,128)(2,1)}, u32[]{:S(2)}, u32[]{:S(2)}) %collective-permute-start.5) | collective-permute-done | bytes 786464 | tf_op jit(solution)/shard_map/ppermute | solution.py:164
  328.7 6.8 %shard_map.115 = bf16[1024,768]{1,0:T(8,128)(2,1)} custom-call(s32[1]{0:T(128)} %bitcast.me_ref, bf16[512,768]{1,0:T(8,128)(2,1)} %shard_map.112.refs_0_, bf16[512,768]{1,0:T(8,128)(2,1)} %collective-permute-done.4.refs_1_, bf16[512,768]{1,0:T(8,128)(2,1)} %collective-permute-done.5.refs_2_, ...), custom_call_target="tpu_custom_call", output_to_operand_aliasing={{}: (9, {})} | custom-call | flops 2415919104 | bytes 9437184 | tf_op jit(solution)/shard_map/pallas_call | solution.py:187
  (63 shorter events, 14.9 us)
Async XLA Ops:
  6.5 99.0 %all-gather.5.cloned.1.call-start = ((), (), s32[]{:S(2)}) async-start(), calls=%async_computation | async-start | bytes 10616832 | tf_op jit(solution)/shard_map/all_gather | solution.py:222
  9.4 1.6 copy-start.6
  10.9 199.6 %all-gather.9.cloned.1.call-start = ((), (), s32[]{:S(2)}) async-start(), calls=%async_computation.2 | async-start | bytes 7077888 | tf_op jit(solution)/shard_map/all_gather | solution.py:248
  59.7 3.7 %copy-start.7 = (bf16[3,3072]{1,0:T(4,128)(2,1)S(1)}, bf16[3,3072]{1,0:T(4,128)(2,1)}, u32[]{:S(2)}) copy-start(bf16[3,3072]{1,0:T(4,128)(2,1)} %param.14) | copy-start | bytes 55300
  63.4 234.5 %all-gather.7.cloned.1.call-start = ((), (), s32[]{:S(2)}) async-start(), calls=%async_computation.1 | async-start | bytes 5308416 | tf_op jit(solution)/shard_map/all_gather | solution.py:262
  67.3 4.8 %copy-start.8 = (bf16[3,768]{1,0:T(4,128)(2,1)S(1)}, bf16[3,768]{1,0:T(4,128)(2,1)}, u32[]{:S(2)}) copy-start(bf16[3,768]{1,0:T(4,128)(2,1)} %param.16) | copy-start | bytes 13828
  117.0 114.7 %collective-permute-start.3 = (bf16[1024,768]{1,0:T(8,128)(2,1)}, bf16[1024,768]{1,0:T(8,128)(2,1)S(1)}, u32[]{:S(2)}, u32[]{:S(2)}) collective-permute-start(bf16[1024,768]{1,0:T(8,128)(2,1)} %shard_map.111.vc), channel_id=1, source_target_pairs={{4,0},{8,4},{12,8},{16,12},{20,16},{24,20},{28,24},{0,28},{5,1},{9... | collective-permute-start | bytes 4718600 | tf_op jit(solution)/shard_map/ppermute | solution.py:267
  117.4 114.3 %collective-permute-start.1 = (bf16[1024,768]{1,0:T(8,128)(2,1)}, bf16[1024,768]{1,0:T(8,128)(2,1)S(1)}, u32[]{:S(2)}, u32[]{:S(2)}) collective-permute-start(bf16[1024,768]{1,0:T(8,128)(2,1)} %shard_map.111.vc), channel_id=1, source_target_pairs={{0,4},{4,8},{8,12},{12,16},{16,20},{20,24},{24,28},{28,0},{1,5},{5... | collective-permute-start | bytes 4718600 | tf_op jit(solution)/shard_map/ppermute | solution.py:266
  130.2 107.4 %collective-permute-start.2 = (bf16[1024,768]{1,0:T(8,128)(2,1)}, bf16[1024,768]{1,0:T(8,128)(2,1)}, u32[]{:S(2)}, u32[]{:S(2)}) collective-permute-start(bf16[1024,768]{1,0:T(8,128)(2,1)} %shard_map.110.kc), channel_id=1, source_target_pairs={{4,0},{8,4},{12,8},{16,12},{20,16},{24,20},{28,24},{0,28},{5,1},{9... | collective-permute-start | bytes 4718600 | tf_op jit(solution)/shard_map/ppermute | solution.py:267
  133.6 109.1 %collective-permute-start = (bf16[1024,768]{1,0:T(8,128)(2,1)}, bf16[1024,768]{1,0:T(8,128)(2,1)}, u32[]{:S(2)}, u32[]{:S(2)}) collective-permute-start(bf16[1024,768]{1,0:T(8,128)(2,1)} %shard_map.110.kc), channel_id=1, source_target_pairs={{0,4},{4,8},{8,12},{12,16},{16,20},{20,24},{24,28},{28,0},{1,5},{5... | collective-permute-start | bytes 4718600 | tf_op jit(solution)/shard_map/ppermute | solution.py:266
  231.7 11.0 %copy-start = (bf16[1024,768]{1,0:T(8,128)(2,1)}, bf16[1024,768]{1,0:T(8,128)(2,1)S(1)}, u32[]{:S(2)}) copy-start(bf16[1024,768]{1,0:T(8,128)(2,1)S(1)} %collective-permute-done.3.vr) | copy-start | bytes 4718596
  231.7 11.0 %copy-start.1 = (bf16[1024,768]{1,0:T(8,128)(2,1)}, bf16[1024,768]{1,0:T(8,128)(2,1)S(1)}, u32[]{:S(2)}) copy-start(bf16[1024,768]{1,0:T(8,128)(2,1)S(1)} %collective-permute-done.1.vl) | copy-start | bytes 4718596
  259.3 22.6 %collective-permute-start.9 = (bf16[512,768]{1,0:T(8,128)(2,1)}, bf16[512,768]{1,0:T(8,128)(2,1)S(1)}, u32[]{:S(2)}, u32[]{:S(2)}) collective-permute-start(bf16[512,768]{1,0:T(8,128)(2,1)} %shard_map.113.refs_0_), channel_id=1, source_target_pairs={{3,0},{2,1},{1,2},{0,3},{7,4},{6,5},{5,6},{4,7},{11,8},{10,9},{9,1... | collective-permute-start | bytes 2359304 | tf_op jit(solution)/shard_map/ppermute | solution.py:164
  261.8 36.0 %collective-permute-start.8 = (bf16[512,768]{1,0:T(8,128)(2,1)}, bf16[512,768]{1,0:T(8,128)(2,1)S(1)}, u32[]{:S(2)}, u32[]{:S(2)}) collective-permute-start(bf16[512,768]{1,0:T(8,128)(2,1)} %shard_map.113.refs_0_), channel_id=1, source_target_pairs={{2,0},{3,1},{0,2},{1,3},{6,4},{7,5},{4,6},{5,7},{10,8},{11,9},{8,1... | collective-permute-start | bytes 2359304 | tf_op jit(solution)/shard_map/ppermute | solution.py:164
  262.4 35.5 %collective-permute-start.7 = (bf16[512,768]{1,0:T(8,128)(2,1)}, bf16[512,768]{1,0:T(8,128)(2,1)S(1)}, u32[]{:S(2)}, u32[]{:S(2)}) collective-permute-start(bf16[512,768]{1,0:T(8,128)(2,1)} %shard_map.113.refs_0_), channel_id=1, source_target_pairs={{1,0},{0,1},{3,2},{2,3},{5,4},{4,5},{7,6},{6,7},{9,8},{8,9},{11,10... | collective-permute-start | bytes 2359304 | tf_op jit(solution)/shard_map/ppermute | solution.py:164
  278.9 35.8 %collective-permute-start.6 = (bf16[512,768]{1,0:T(8,128)(2,1)}, bf16[512,768]{1,0:T(8,128)(2,1)S(1)}, u32[]{:S(2)}, u32[]{:S(2)}) collective-permute-start(bf16[512,768]{1,0:T(8,128)(2,1)} %shard_map.112.refs_0_), channel_id=1, source_target_pairs={{3,0},{2,1},{1,2},{0,3},{7,4},{6,5},{5,6},{4,7},{11,8},{10,9},{9,1... | collective-permute-start | bytes 2359304 | tf_op jit(solution)/shard_map/ppermute | solution.py:164
  281.4 47.3 %collective-permute-start.5 = (bf16[512,768]{1,0:T(8,128)(2,1)}, bf16[512,768]{1,0:T(8,128)(2,1)}, u32[]{:S(2)}, u32[]{:S(2)}) collective-permute-start(bf16[512,768]{1,0:T(8,128)(2,1)} %shard_map.112.refs_0_), channel_id=1, source_target_pairs={{2,0},{3,1},{0,2},{1,3},{6,4},{7,5},{4,6},{5,7},{10,8},{11,9},{8,1... | collective-permute-start | bytes 2359304 | tf_op jit(solution)/shard_map/ppermute | solution.py:164
  281.9 16.0 %copy-start.2 = (bf16[512,768]{1,0:T(8,128)(2,1)}, bf16[512,768]{1,0:T(8,128)(2,1)S(1)}, u32[]{:S(2)}) copy-start(bf16[512,768]{1,0:T(8,128)(2,1)S(1)} %collective-permute-done.9.refs_3_) | copy-start | bytes 2359300
  281.9 46.7 %collective-permute-start.4 = (bf16[512,768]{1,0:T(8,128)(2,1)}, bf16[512,768]{1,0:T(8,128)(2,1)}, u32[]{:S(2)}, u32[]{:S(2)}) collective-permute-start(bf16[512,768]{1,0:T(8,128)(2,1)} %shard_map.112.refs_0_), channel_id=1, source_target_pairs={{1,0},{0,1},{3,2},{2,3},{5,4},{4,5},{7,6},{6,7},{9,8},{8,9},{11,10... | collective-permute-start | bytes 2359304 | tf_op jit(solution)/shard_map/ppermute | solution.py:164
  297.8 0.9 copy-start.3
  297.9 1.1 copy-start.5
  314.7 14.0 %copy-start.4 = (bf16[512,768]{1,0:T(8,128)(2,1)}, bf16[512,768]{1,0:T(8,128)(2,1)S(1)}, u32[]{:S(2)}) copy-start(bf16[512,768]{1,0:T(8,128)(2,1)S(1)} %collective-permute-done.6.refs_3_) | copy-start | bytes 2359300
Sparse Core Ops, SparseCore 0:
  11.0 94.4 all-gather.4
  107.1 103.3 all-gather.8
  212.1 63.2 all-gather.6
